TPU v7x, 256 devices: a whole 4x4x8 slice. The times are simulated.
256 devices in a mesh: ctx: 8 (over z_hi, core), exp: 32 (over x, z_lo, y).
Axes of the slice: x: 4, y: 4, z: 8 (z_hi: 4, z_lo: 2; z = z_hi * 2 + z_lo), core: 2. Of those that a mesh axis runs over, the one named last changes fastest.
Arguments:
- queries: bfloat16 [4096, 4096], P('ctx', 'exp'), may hold values from -8 to 8
- doc_keys: bfloat16 [8192, 4096], P('ctx', 'exp'), may hold values from -8 to 8
- doc_values: bfloat16 [8192, 4096], P('ctx', 'exp'), may hold values from -6 to 6
- residual: bfloat16 [4096, 4096], P(('ctx', 'exp')), may hold values from -3 to 3
- out_weight: bfloat16 [4096, 4096], P('exp'), may hold values from -0.09375 to 0.09375
- norm_gain: float32 [4096], replicated, may hold values from 0.1 to 1.9
- expert_ids: int32 [4096, 1], P(('ctx', 'exp')), may hold values from 0 to 7; in each aligned block of 16 rows (0 to 15, 16 to 31, ...) at most 4 rows name the same one
- gate_up: bfloat16 [32, 4096, 5120], P('exp', None, 'ctx'), may hold values from -0.09375 to 0.09375
- down_weight: bfloat16 [32, 2560, 4096], P('exp', 'ctx'), may hold values from -0.0625 to 0.0625
Outputs:
- attended: bfloat16 [4096, 4096], P(('ctx', 'exp'))
- expert_out: bfloat16 [4096, 4096], P(('ctx', 'exp'))
Inputs may be any that keep to these rules, and one draw needn't show every extreme that they name: `expert_ids`: in each aligned block of 16 tokens, the rows of one device, no expert is named more than 4 times.
All inputs are finite; a program needn't handle non-finite values.
Results may differ from a plain program's by a relative error of at most 0.033.
Values may be sent and summed in bfloat16 or wider, within the bound.
No kernel may reach another device: no remote copies, remote signals or barrier semaphores. Data moves between devices by JAX's collectives and lax.ppermute only.
A program may use at most 128 MiB of HBM per device.

v0:
```python
import functools

import jax
import jax.numpy as jnp
from jax import lax
from jax.experimental import pallas as pl
from jax.experimental.pallas import tpu as pltpu
from jax.sharding import Mesh
from jax.sharding import PartitionSpec as P

DH = 64
CAP = 4
CTX = ("zhi", "core")
EXP = ("x", "zlo", "y")
PLANE = ("zhi", "zlo", "x")
INTERPRET = False


X_STEPS = (0, 1, -1, 2)
DEEP = 512


def shift(value, axis, step):
    size = lax.axis_size(axis)
    return lax.ppermute(value, axis, [(i, (i + step) % size) for i in range(size)])


def swap(value):
    return shift(value, "core", 1)


def in_vmem(value):
    return value if INTERPRET else pltpu.with_memory_space_constraint(value, pltpu.VMEM)


def attend_kernel(count, first, last, *refs):
    q_ref, keys, values = refs[0], refs[1 : 1 + count], refs[1 + count : 1 + 2 * count]
    rest = refs[1 + 2 * count :]
    if not first:
        acc_in, top_in, total_in = rest[:3]
        rest = rest[3:]
    head = pl.program_id(1)
    queries = q_ref[...]
    mine = lax.broadcasted_iota(jnp.int32, queries.shape, 1) // DH == head
    own = jnp.where(mine, queries, jnp.zeros_like(queries)) * jnp.asarray(DH**-0.5, queries.dtype)
    if first:
        top = jnp.full((queries.shape[0], 1), -jnp.inf, jnp.float32)
        total = jnp.zeros((queries.shape[0], 1), jnp.float32)
        acc = jnp.zeros(queries.shape, jnp.float32)
    else:
        top = jnp.max(jnp.where(mine, top_in[...], -jnp.inf), axis=1, keepdims=True)
        total = jnp.max(jnp.where(mine, total_in[...], 0.0), axis=1, keepdims=True)
        acc = acc_in[...]
    for key, value in zip(keys, values):
        scores = lax.dot_general(
            own, key[...], (((1,), (1,)), ((), ())), preferred_element_type=jnp.float32
        )
        new_top = jnp.maximum(top, jnp.max(scores, axis=1, keepdims=True))
        decay = jnp.exp(top - new_top)
        weights = jnp.exp(scores - new_top)
        total = total * decay + jnp.sum(weights, axis=1, keepdims=True)
        acc = acc * decay + jnp.dot(
            weights.astype(jnp.bfloat16), value[...], preferred_element_type=jnp.float32
        )
        top = new_top
    if last:
        results = ((acc / total).astype(jnp.bfloat16),)
    else:
        results = (acc, jnp.broadcast_to(top, acc.shape), jnp.broadcast_to(total, acc.shape))

    @pl.when(head == 0)
    def _():
        for ref, result in zip(rest, results):
            ref[...] = result

    @pl.when(head != 0)
    def _():
        for ref, result in zip(rest, results):
            ref[...] = jnp.where(mine, result, ref[...])


def attend(queries, keys, values, state, last):
    total_rows, width = queries.shape
    rows = min(128, total_rows)
    heads = width // DH
    whole = [pl.BlockSpec(k.shape, lambda i, h: (0, 0)) for k in keys + values]
    part = pl.BlockSpec((rows, width), lambda i, h: (i, 0))
    docs = sum(k.shape[0] for k in keys)
    if last:
        shapes = [jax.ShapeDtypeStruct(queries.shape, jnp.bfloat16)]
    else:
        shapes = [jax.ShapeDtypeStruct(queries.shape, jnp.float32)] * 3
    return pl.pallas_call(
        functools.partial(attend_kernel, len(keys), not state, last),
        grid=(total_rows // rows, heads),
        in_specs=[part] + whole + [part] * len(state),
        out_specs=[part] * len(shapes),
        out_shape=shapes,
        cost_estimate=pl.CostEstimate(
            flops=4 * total_rows * docs * width,
            bytes_accessed=4 * docs * width + 14 * total_rows * width,
            transcendentals=heads * total_rows * docs,
        ),
        interpret=INTERPRET,
    )(queries, *keys, *values, *state)


def attention(queries, keys, values, early):
    near_keys = [swap(keys), shift(keys, "zhi", 1), shift(keys, "zhi", -1)]
    near_values = [swap(values), shift(values, "zhi", 1), shift(values, "zhi", -1)]
    state = attend(queries, [keys, near_keys[0]], [values, near_values[0]], [], False)
    far_key = shift(near_keys[1], "zhi", 1)
    far_value = shift(near_values[2], "zhi", -1)
    state = attend(
        queries,
        near_keys[1:] + [swap(k) for k in near_keys[1:]],
        near_values[1:] + [swap(v) for v in near_values[1:]],
        state,
        False,
    )
    state, far_key, far_value, early = lax.optimization_barrier((state, far_key, far_value, early))
    (context,) = attend(queries, [far_key, swap(far_key)], [far_value, swap(far_value)], state, True)
    return context, early


def pack_kernel(residual_ref, ids_ref, weight_ref, out_ref):
    wide, chunk = weight_ref.shape[0], weight_ref.shape[1] // out_ref.shape[0]
    rest = out_ref.shape[2] - chunk
    rows = residual_ref.shape[0]
    ids = jnp.broadcast_to(ids_ref[...].astype(jnp.float32), (rows, rest)).astype(jnp.bfloat16)
    for part in range(out_ref.shape[0]):
        at = slice(part * chunk, (part + 1) * chunk)
        out_ref[part, :wide, :chunk] = weight_ref[:, at]
        out_ref[part, :wide, chunk:] = jnp.zeros((wide, rest), jnp.bfloat16)
        out_ref[part, wide:, :chunk] = residual_ref[:, at]
        out_ref[part, wide:, chunk:] = ids


def pack(residual, ids, weight):
    nx = lax.axis_size("x")
    shape = (nx, weight.shape[0] + residual.shape[0], weight.shape[1] // nx + 128)
    return pl.pallas_call(
        pack_kernel,
        in_specs=[pl.BlockSpec(memory_space=pltpu.VMEM)] * 3,
        out_shape=jax.ShapeDtypeStruct(shape, jnp.bfloat16),
        cost_estimate=pl.CostEstimate(
            flops=0, bytes_accessed=4 * weight.shape[0] * weight.shape[1], transcendentals=0
        ),
        name="pack",
        interpret=INTERPRET,
    )(residual, ids, weight)


def choose_kernel(nx, nzlo, got_ref, residual_ref, chosen_ref):
    rows, chunk = got_ref.shape[1], residual_ref.shape[1]
    tokens = nx * rows
    for part in range(nx):
        residual_ref[part * rows : (part + 1) * rows] = got_ref[part, :, :chunk]
    ids = [got_ref[part, :, chunk : chunk + tokens].astype(jnp.float32) for part in range(nx)]
    by_row = jnp.concatenate(ids, axis=0)
    row = lax.broadcasted_iota(jnp.int32, (tokens, tokens), 0)
    column = lax.broadcasted_iota(jnp.int32, (tokens, tokens), 1)
    by_column = jnp.sum(jnp.where(row == column, by_row, 0.0), axis=0, keepdims=True)
    earlier = (by_row == by_column) & (row // rows == column // rows) & (row < column)
    rank = jnp.sum(earlier.astype(jnp.float32), axis=0, keepdims=True)
    slots = chosen_ref.shape[0]
    row = lax.broadcasted_iota(jnp.int32, (slots, tokens), 0)
    column = lax.broadcasted_iota(jnp.int32, (slots, tokens), 1)
    plane = row // (nx * CAP)
    expert = (plane % nx * nzlo + plane // nx).astype(jnp.float32)
    chosen = (
        (by_column == expert)
        & (rank == (row % CAP).astype(jnp.float32))
        & (row // CAP % nx == column // rows)
    )
    chosen_ref[...] = chosen.astype(jnp.bfloat16)


def choose(payload, rows, chunk, nx, nzlo):
    high = payload.shape[1] // rows - 1
    shapes = [(nx * rows, chunk), (nx * nzlo * nx * CAP, nx * rows)]
    return pl.pallas_call(
        functools.partial(choose_kernel, nx, nzlo),
        grid=(1,),
        in_specs=[pl.BlockSpec((nx, rows, payload.shape[2]), lambda i: (0, high, 0))],
        out_specs=[pl.BlockSpec(shape, lambda i: (0, 0)) for shape in shapes],
        out_shape=[jax.ShapeDtypeStruct(shape, jnp.bfloat16) for shape in shapes],
        cost_estimate=pl.CostEstimate(flops=10**7, bytes_accessed=4 * shapes[0][0] * chunk, transcendentals=0),
        name="choose",
        interpret=INTERPRET,
    )(payload)


def project_kernel(chunk, x_ref, payload_ref, *refs):
    contexts, out_ref = refs[:-1], refs[-1]
    nx, width = len(contexts), contexts[0].shape[1]
    context = jnp.concatenate([r[...] for r in contexts], axis=1)
    weights = [payload_ref[(x_ref[0] - step + nx) % nx, :width, :chunk] for step in X_STEPS]
    weight = jnp.concatenate(weights, axis=0)
    out_ref[...] = jnp.dot(context, weight, preferred_element_type=jnp.float32).astype(jnp.bfloat16)


def project(at_x, contexts, payload, chunk):
    rows, width = contexts[0].shape
    part = min(256, rows)
    count = len(contexts)
    return pl.pallas_call(
        functools.partial(project_kernel, chunk),
        grid=(rows // part,),
        in_specs=[pl.BlockSpec(memory_space=pltpu.SMEM), pl.BlockSpec(payload.shape, lambda i: (0, 0, 0))]
        + [pl.BlockSpec((part, width), lambda i: (i, 0))] * count,
        out_specs=pl.BlockSpec((part, chunk), lambda i: (i, 0)),
        out_shape=jax.ShapeDtypeStruct((rows, chunk), jnp.bfloat16),
        cost_estimate=pl.CostEstimate(
            flops=2 * rows * width * count * chunk,
            bytes_accessed=2 * (rows * width * count + width * count * chunk + rows * chunk),
            transcendentals=0,
        ),
        name="project",
        interpret=INTERPRET,
    )(at_x, payload, *contexts)


def norm_kernel(groups, chunks, in_ref, gain_ref, out_ref):
    rows, chunk = in_ref.shape[1:]
    for group in range(groups):
        parts = [in_ref[group * chunks + i].astype(jnp.float32) for i in range(chunks)]
        squares = sum(jnp.sum(p * p, axis=1, keepdims=True) for p in parts)
        scale = lax.rsqrt(squares * (1.0 / (chunks * chunk)) + 1e-06)
        for i, p in enumerate(parts):
            gain = gain_ref[:, i * chunk : (i + 1) * chunk]
            out_ref[group * rows : (group + 1) * rows, i * chunk : (i + 1) * chunk] = (
                p * scale * gain
            ).astype(jnp.bfloat16)


def norm_rows(incoming, gain, groups, chunks):
    rows, chunk = incoming.shape[1:]
    shape = (groups * rows, chunks * chunk)
    return pl.pallas_call(
        functools.partial(norm_kernel, groups, chunks),
        in_specs=[pl.BlockSpec(memory_space=pltpu.VMEM)] * 2,
        out_shape=jax.ShapeDtypeStruct(shape, jnp.bfloat16),
        cost_estimate=pl.CostEstimate(
            flops=4 * shape[0] * shape[1], bytes_accessed=4 * shape[0] * shape[1], transcendentals=shape[0]
        ),
        name="norm_rows",
        interpret=INTERPRET,
    )(in_vmem(incoming), gain[None, :])


def expert_kernel(count, *refs):
    own, other = refs[:count], refs[count : 2 * count]
    gate_up, down, own_out, other_out, acc = refs[2 * count :]
    step = pl.program_id(0)
    rows = jnp.concatenate([r[...] for r in own + other], axis=0)

    @pl.when(step == 0)
    def _():
        acc[...] = jnp.zeros(acc.shape, jnp.float32)

    acc[...] += jnp.dot(rows, gate_up[...], preferred_element_type=jnp.float32)

    @pl.when(step == pl.num_programs(0) - 1)
    def _():
        width = down.shape[0]
        half = own_out.shape[0]
        gate = acc[:, :width]
        hidden = (gate / (1.0 + jnp.exp(-gate)) * acc[:, width:]).astype(jnp.bfloat16)
        part = min(512, down.shape[1])

        def columns(i, carry):
            at = pl.ds(pl.multiple_of(i * part, part), part)
            out = jnp.dot(hidden, down[:, at], preferred_element_type=jnp.float32).astype(jnp.bfloat16)
            own_out[:, at] = out[:half]
            other_out[:, at] = out[half:]
            return carry

        lax.fori_loop(0, down.shape[1] // part, columns, 0)


def expert_block(own, other, gate_up, down_weight):
    count = len(own)
    rows, width = own[0].shape
    deep = min(DEEP, width)
    total = 2 * count * rows
    block = pl.BlockSpec((rows, deep), lambda i: (0, i))
    shape = (count * rows, width)
    whole = pl.BlockSpec(shape, lambda i: (0, 0))
    out_own, out_other = pl.pallas_call(
        functools.partial(expert_kernel, count),
        grid=(width // deep,),
        in_specs=[block] * (2 * count)
        + [pl.BlockSpec((deep, gate_up.shape[1]), lambda i: (i, 0)), pl.BlockSpec(down_weight.shape, lambda i: (0, 0))],
        out_specs=[whole, whole],
        out_shape=[jax.ShapeDtypeStruct(shape, jnp.bfloat16)] * 2,
        scratch_shapes=[pltpu.VMEM((total, gate_up.shape[1]), jnp.float32)],
        cost_estimate=pl.CostEstimate(
            flops=2 * total * (gate_up.size + down_weight.size),
            bytes_accessed=2 * (gate_up.size + down_weight.size + 2 * total * width),
            transcendentals=total * down_weight.shape[0],
        ),
        interpret=INTERPRET,
    )(*own, *other, gate_up, down_weight)
    return add_rounded(out_own, swap(out_other))


def add_rounded(a, b):
    return (a.astype(jnp.float32) + b.astype(jnp.float32)).astype(jnp.bfloat16)


def last_sum_kernel(own_ref, low_a, low_b, high_a, high_b, out_ref):
    half = low_a.shape[0]
    wide = own_ref.shape[1] // 2
    for start, first, second in ((0, low_a, low_b), (half, high_a, high_b)):
        for at in range(0, half, CAP):
            rows = slice(start + at, start + at + CAP)
            whole = (
                own_ref[rows].astype(jnp.float32)
                + first[at : at + CAP].astype(jnp.float32)
                + second[at : at + CAP].astype(jnp.float32)
            )
            both = jnp.concatenate([whole[:, :wide], whole[:, wide:]], axis=0)
            out_ref[(start + at) // CAP] = both.astype(jnp.bfloat16)


def last_sum(own, low_a, low_b, high_a, high_b):
    rows, width = own.shape
    shape = (rows // CAP, 2 * CAP, width // 2)
    return pl.pallas_call(
        last_sum_kernel,
        out_shape=jax.ShapeDtypeStruct(shape, jnp.bfloat16),
        cost_estimate=pl.CostEstimate(
            flops=2 * rows * width, bytes_accessed=8 * rows * width, transcendentals=0
        ),
        name="last_sum",
        interpret=INTERPRET,
    )(own, low_a, low_b, high_a, high_b)


def combine_kernel(picked_ref, returned_ref, out_ref):
    rows, wide = out_ref.shape[0], returned_ref.shape[1]
    both = jnp.dot(picked_ref[...], returned_ref[...], preferred_element_type=jnp.float32)
    for half in range(2):
        out_ref[:, half * wide : (half + 1) * wide] = both[half * rows : (half + 1) * rows].astype(
            jnp.bfloat16
        )


def combine(picked, returned):
    shape = (picked.shape[0] // 2, 2 * returned.shape[1])
    return pl.pallas_call(
        combine_kernel,
        in_specs=[pl.BlockSpec(memory_space=pltpu.VMEM)] * 2,
        out_shape=jax.ShapeDtypeStruct(shape, jnp.bfloat16),
        cost_estimate=pl.CostEstimate(
            flops=2 * picked.shape[0] * returned.size,
            bytes_accessed=2 * (returned.size + shape[0] * shape[1]),
            transcendentals=0,
        ),
        name="combine",
        interpret=INTERPRET,
    )(picked, in_vmem(returned))


def on_device(
    queries, doc_keys, doc_values, residual, out_weight, norm_gain, expert_ids, gate_up, down_weight
):
    nx, nzlo, ny, nzhi = (lax.axis_size(a) for a in ("x", "zlo", "y", "zhi"))
    rows, width = residual.shape
    chunk = width // nx
    group = nzlo * ny
    experts = nx * nzlo

    at_x = lax.axis_index("x").astype(jnp.int32).reshape(1)
    ordered = queries.reshape(nx, group, rows, -1).transpose(1, 0, 2, 3).reshape(queries.shape)
    sent = pack(residual, expert_ids, out_weight)
    payload = lax.all_to_all(sent, "x", split_axis=0, concat_axis=0, tiled=True)
    residual_chunk, chosen = choose(payload, rows, chunk, nx, nzlo)
    context, (payload, residual_chunk, chosen) = attention(
        ordered, doc_keys, doc_values, (payload, residual_chunk, chosen)
    )
    contexts = [context] + [shift(context, "x", step) for step in X_STEPS[1:]]
    partial_rows = project(at_x, contexts, payload, chunk)
    pieces = lax.all_to_all(
        partial_rows.reshape(group, nx * rows, chunk), ("zlo", "y"), split_axis=0, concat_axis=0, tiled=True
    )
    mixed = jnp.sum(pieces.astype(jnp.float32), axis=0)
    attended_chunk = (residual_chunk.astype(jnp.float32) + mixed).astype(jnp.bfloat16)
    attended = lax.all_to_all(attended_chunk, "x", split_axis=0, concat_axis=1, tiled=True)

    outgoing = jnp.dot(chosen, attended_chunk, preferred_element_type=jnp.float32).astype(jnp.bfloat16)
    outgoing = outgoing.reshape(1, experts, nx * CAP, chunk)
    outgoing = jnp.broadcast_to(outgoing, (nzhi,) + outgoing.shape[1:]).reshape(
        nzhi * experts, nx * CAP, chunk
    )
    incoming = lax.all_to_all(outgoing, PLANE, split_axis=0, concat_axis=0, tiled=True)
    normed = norm_rows(incoming, norm_gain, nzhi * nzlo, nx)

    half = normed.shape[0] // 2
    gate_up, down_weight = gate_up[0], down_weight[0]
    from_prev, from_next = shift(normed, "y", 1), shift(normed, "y", -1)
    sum_own = expert_block([normed], [swap(normed)], gate_up, down_weight)
    far_up = shift(from_prev[:half], "y", 1)
    far_down = shift(from_next[half:], "y", -1)
    sides = [from_prev, from_next]
    sum_side = expert_block(sides, [swap(r) for r in sides], gate_up, down_weight)
    prev_low, prev_high, next_low, next_high = (sum_side[i * half : (i + 1) * half] for i in range(4))
    early_next, early_prev = shift(next_high, "y", 1), shift(prev_low, "y", -1)
    far = jnp.concatenate([far_up, far_down], axis=0)
    sum_far = expert_block([far], [swap(far)], gate_up, down_weight)
    relay_next, relay_prev = shift(sum_far[:half], "y", 1), shift(sum_far[half:], "y", -1)
    late_next = shift(add_rounded(next_low, relay_next), "y", 1)
    late_prev = shift(add_rounded(prev_high, relay_prev), "y", -1)
    summed = last_sum(sum_own, late_next, early_prev, early_next, late_prev)
    returned = lax.all_to_all(summed, PLANE, split_axis=0, concat_axis=0, tiled=True)
    own_routes = expert_ids[:, 0]
    positions = jnp.arange(rows, dtype=jnp.int32)
    slots = jnp.arange(CAP, dtype=jnp.int32)
    expert_of = (
        jnp.arange(nx, dtype=jnp.int32)[None, :] * nzlo + jnp.arange(nzlo, dtype=jnp.int32)[:, None]
    ).reshape(-1)
    own_earlier = (own_routes[:, None] == own_routes[None, :]) & (positions[:, None] > positions[None, :])
    own_rank = jnp.sum(own_earlier.astype(jnp.int32), axis=1)
    picked = (own_routes[:, None, None] == expert_of[None, :, None]) & (
        own_rank[:, None, None] == slots[None, None, :]
    )
    halves = jnp.arange(2, dtype=jnp.int32)
    picked = (halves[:, None] == halves[None, :])[:, None, None, None, :, None] & jnp.broadcast_to(
        picked[None, :, None, :, None, :], (1, rows, nzhi, nx * nzlo, 1, CAP)
    )
    expert_sum = combine(
        picked.reshape(2 * rows, -1).astype(jnp.bfloat16), returned.reshape(-1, width // 2)
    )
    return (attended, expert_sum)


def solution(mesh):
    split = Mesh(mesh.devices.reshape(4, 2, 4, 2, 4), CTX + EXP)
    return jax.shard_map(
        on_device,
        mesh=split,
        in_specs=(
            P(CTX, EXP),
            P(CTX, EXP),
            P(CTX, EXP),
            P(CTX + EXP, None),
            P(EXP, None),
            P(),
            P(CTX + EXP, None),
            P(EXP, None, CTX),
            P(EXP, CTX, None),
        ),
        out_specs=(P(CTX + EXP, None), P(CTX + EXP, None)),
        check_vma=False,
    )
```

profile of v0, /device:TPU:8, one launch (start us, length us, event | category | flops | bytes accessed | tf_op | source)
XLA Modules:
  0.0 323.7 jit_solution(11368134065585590752)
XLA Ops:
  2.0 2.6 pack.1
  4.5 4.3 %all-to-all-start = ((bf16[4,144,1152]{2,1,0:T(8,128)(2,1)}), bf16[4,144,1152]{2,1,0:T(8,128)(2,1)S(1)}, u32[]{:S(2)}, u32[]{:S(2)}) async-start(bf16[4,144,1152]{2,1,0:T(8,128)(2,1)} %pack.1), calls=%async_computation | async-start | bytes 2654208 | tf_op jit(solution)/shard_map/all_to_all | solution.py:378
  8.8 3.3 %collective-permute-start = (bf16[1024,128]{1,0:T(8,128)(2,1)S(1)}, bf16[1024,128]{1,0:T(8,128)(2,1)S(1)}, u32[]{:S(2)}, u32[]{:S(2)}) collective-permute-start(bf16[1024,128]{1,0:T(8,128)(2,1)S(1)} %copy-done.17), channel_id=1, source_target_pairs={{0,64},{64,128},{128,192},{192,0},{1,65},{65,129},{129,193},{193,1... | collective-permute-start | bytes 786440 | tf_op jit(solution)/shard_map/ppermute | solution.py:25
  12.2 3.1 collective-permute-start.5
  15.3 2.8 collective-permute-start.1
  18.2 6.1 %collective-permute-done.refs_1_ = bf16[1024,128]{1,0:T(8,128)(2,1)S(1)} collective-permute-done((bf16[1024,128]{1,0:T(8,128)(2,1)S(1)}, bf16[1024,128]{1,0:T(8,128)(2,1)S(1)}, u32[]{:S(2)}, u32[]{:S(2)}) %collective-permute-start) | collective-permute-done | bytes 262176 | tf_op jit(solution)/shard_map/ppermute | solution.py:25
  24.4 10.7 %collective-permute-done.5.refs_6_ = bf16[1024,128]{1,0:T(8,128)(2,1)S(1)} collective-permute-done((bf16[1024,128]{1,0:T(8,128)(2,1)S(1)}, bf16[1024,128]{1,0:T(8,128)(2,1)S(1)}, u32[]{:S(2)}, u32[]{:S(2)}) %collective-permute-start.5) | collective-permute-done | bytes 262176 | tf_op jit(solution)/shard_map/ppermute | solution.py:25
  35.0 5.1 %collective-permute-done.1.refs_2_ = bf16[1024,128]{1,0:T(8,128)(2,1)S(1)} collective-permute-done((bf16[1024,128]{1,0:T(8,128)(2,1)S(1)}, bf16[1024,128]{1,0:T(8,128)(2,1)S(1)}, u32[]{:S(2)}, u32[]{:S(2)}) %collective-permute-start.1) | collective-permute-done | bytes 262176 | tf_op jit(solution)/shard_map/ppermute | solution.py:25
  40.7 3.7 %collective-permute-start.10 = (bf16[1024,128]{1,0:T(8,128)(2,1)S(1)}, bf16[1024,128]{1,0:T(8,128)(2,1)S(1)}, u32[]{:S(2)}, u32[]{:S(2)}) collective-permute-start(bf16[1024,128]{1,0:T(8,128)(2,1)S(1)} %collective-permute-done.refs_1_), channel_id=1, source_target_pairs={{0,64},{64,128},{128,192},{192,0},{1,65},{65,129},{129,193},{193,1... | collective-permute-start | bytes 786440 | tf_op jit(solution)/shard_map/ppermute | solution.py:25
  45.5 9.1 %shard_map.107 = (f32[512,128]{1,0:T(8,128)}, f32[512,128]{1,0:T(8,128)}, f32[512,128]{1,0:T(8,128)}) custom-call(bf16[512,128]{1,0:T(8,128)(2,1)} %bitcast.33, bf16[1024,128]{1,0:T(8,128)(2,1)} %refs_1_.1, bf16[1024,128]{1,0:T(8,128)(2,1)} %copy-done.23, bf16[1024,128]{1,0:T(8,128)(2,1)} %refs_3_.1, bf16[1024,128]{1,0:T(8,128)(2,1)} %copy-done.27), custom_call_target="tpu_custom_call" | custom-call | flops 536870912 | bytes 1966080 | tf_op jit(solution)/shard_map/pallas_call | solution.py:93
  54.7 15.2 %shard_map.108 = (f32[512,128]{1,0:T(8,128)}, f32[512,128]{1,0:T(8,128)}, f32[512,128]{1,0:T(8,128)}) custom-call(bf16[512,128]{1,0:T(8,128)(2,1)} %bitcast.34, bf16[1024,128]{1,0:T(8,128)(2,1)} %copy-done.19, bf16[1024,128]{1,0:T(8,128)(2,1)} %copy-done.21, bf16[1024,128]{1,0:T(8,128)(2,1)} %copy-done.26, bf16[1024,128]{1,0:T(8,128)(2,1)} %collective-permute-done.3.refs_4_, ...), custom_call_target="tpu_custom_call" | custom-call | flops 1073741824 | bytes 3014656 | tf_op jit(solution)/shard_map/pallas_call | solution.py:93
  75.6 9.2 %shard_map.109.refs_0_ = bf16[512,128]{1,0:T(8,128)(2,1)} custom-call(bf16[512,128]{1,0:T(8,128)(2,1)} %bitcast.35, bf16[1024,128]{1,0:T(8,128)(2,1)} %copy-done.24, bf16[1024,128]{1,0:T(8,128)(2,1)} %copy-done.28, bf16[1024,128]{1,0:T(8,128)(2,1)} %copy-done.25, bf16[1024,128]{1,0:T(8,128)(2,1)} %copy-done.29, f32[512,128]{1,0:T(8,128)} %get-tuple-element.36.refs_5_, ...), custom_call_target="tpu_custom_call" | custom-call | flops 536870912 | bytes 1966080 | tf_op jit(solution)/shard_map/pallas_call | solution.py:93
  84.8 2.0 collective-permute-start.14
  88.1 2.2 collective-permute-start.16
  93.3 2.7 collective-permute-done.16.refs_3_
  96.7 3.2 project.1
  99.9 18.3 %all_to_all.39 = bf16[8,64,1024]{2,1,0:T(8,128)(2,1)S(1)} all-to-all(bf16[8,64,1024]{2,1,0:T(8,128)(2,1)} %bitcast.28), channel_id=1, replica_groups=mesh['zhi'=4,'core'=2,'x'=4,'zlo'=2,'y'=4] {'zlo','y'}, dimensions={0} | all-to-all | bytes 2097152 | tf_op jit(solution)/shard_map/all_to_all | solution.py:385
  120.4 32.9 %all_to_all.40.in_ref = bf16[32,16,1024]{2,1,0:T(8,128)(2,1)S(1)} all-to-all(bf16[32,16,1024]{2,1,0:T(8,128)(2,1)S(1)} %bitcast.29), channel_id=1, replica_groups=mesh['zhi'=4,'core'=2,'x'=4,'zlo'=2,'y'=4] {'zhi','zlo','x'}, dimensions={0} | all-to-all | bytes 2097152 | tf_op jit(solution)/shard_map/all_to_all | solution.py:397
  153.2 2.2 norm_rows.1.refs_0_
  157.4 20.4 %collective-permute-done.19.refs_0_ = bf16[128,4096]{1,0:T(8,128)(2,1)} collective-permute-done((bf16[128,4096]{1,0:T(8,128)(2,1)}, bf16[128,4096]{1,0:T(8,128)(2,1)}, u32[]{:S(2)}, u32[]{:S(2)}) %collective-permute-start.19) | collective-permute-done | bytes 1048608 | tf_op jit(solution)/shard_map/ppermute | solution.py:25
  182.1 6.0 %collective-permute-done.24 = bf16[64,4096]{1,0:T(8,128)(2,1)S(1)} collective-permute-done((bf16[64,4096]{1,0:T(8,128)(2,1)S(1)}, bf16[64,4096]{1,0:T(8,128)(2,1)S(1)}, u32[]{:S(2)}, u32[]{:S(2)}) %collective-permute-start.24) | collective-permute-done | bytes 524320 | tf_op jit(solution)/shard_map/ppermute | solution.py:25
  193.3 11.8 %shard_map.112 = (bf16[128,4096]{1,0:T(8,128)(2,1)}, bf16[128,4096]{1,0:T(8,128)(2,1)}) custom-call(bf16[128,4096]{1,0:T(8,128)(2,1)} %copy-done.2, bf16[128,4096]{1,0:T(8,128)(2,1)} %copy-done.5, bf16[4096,640]{1,0:T(8,128)(2,1)} %bitcast.22, bf16[320,4096]{1,0:T(8,128)(2,1)} %bitcast.25), custom_call_target="tpu_custom_call" | custom-call | flops 2013265920 | bytes 12058624 | tf_op jit(solution)/shard_map/pallas_call | solution.py:290
  205.3 5.2 %all-to-all-start.2 = ((bf16[4,16,1024]{2,1,0:T(8,128)(2,1)}), bf16[4,16,1024]{2,1,0:T(8,128)(2,1)S(1)}, u32[]{:S(2)}, u32[]{:S(2)}) async-start(bf16[4,16,1024]{2,1,0:T(8,128)(2,1)} %bitcast.6), calls=%async_computation.2 | async-start | bytes 262144 | tf_op jit(solution)/shard_map/all_to_all | solution.py:390
  210.5 15.3 %shard_map.111 = (bf16[256,4096]{1,0:T(8,128)(2,1)}, bf16[256,4096]{1,0:T(8,128)(2,1)}) custom-call(bf16[128,4096]{1,0:T(8,128)(2,1)} %collective-permute-done.19.refs_0_, bf16[128,4096]{1,0:T(8,128)(2,1)} %collective-permute-done.20.refs_1_, bf16[128,4096]{1,0:T(8,128)(2,1)} %collective-permute-done.21.refs_2_, ...), custom_call_target="tpu_custom_call" | custom-call | flops 4026531840 | bytes 16252928 | tf_op jit(solution)/shard_map/pallas_call | solution.py:290
  225.9 11.7 %shard_map.110 = (bf16[128,4096]{1,0:T(8,128)(2,1)}, bf16[128,4096]{1,0:T(8,128)(2,1)}) custom-call(bf16[128,4096]{1,0:T(8,128)(2,1)} %norm_rows.1.refs_0_, bf16[128,4096]{1,0:T(8,128)(2,1)} %collective-permute-done.17.refs_1_, bf16[4096,640]{1,0:T(8,128)(2,1)} %bitcast.24, bf16[320,4096]{1,0:T(8,128)(2,1)} %bitcast.27), custom_call_target="tpu_custom_call" | custom-call | flops 2013265920 | bytes 12058624 | tf_op jit(solution)/shard_map/pallas_call | solution.py:290
  243.0 11.1 %collective-permute-done.28 = bf16[64,4096]{1,0:T(8,128)(2,1)S(1)} collective-permute-done((bf16[64,4096]{1,0:T(8,128)(2,1)S(1)}, bf16[64,4096]{1,0:T(8,128)(2,1)S(1)}, u32[]{:S(2)}, u32[]{:S(2)}) %collective-permute-start.28) | collective-permute-done | bytes 524320 | tf_op jit(solution)/shard_map/ppermute | solution.py:25
  258.4 2.2 collective-permute-start.30
  261.8 9.3 %collective-permute-done.29.low_a = bf16[64,4096]{1,0:T(8,128)(2,1)S(1)} collective-permute-done((bf16[64,4096]{1,0:T(8,128)(2,1)S(1)}, bf16[64,4096]{1,0:T(8,128)(2,1)S(1)}, u32[]{:S(2)}, u32[]{:S(2)}) %collective-permute-start.29) | collective-permute-done | bytes 524320 | tf_op jit(solution)/shard_map/ppermute | solution.py:25
  272.8 8.9 %collective-permute-done.30.low_b = bf16[64,4096]{1,0:T(8,128)(2,1)S(1)} collective-permute-done((bf16[64,4096]{1,0:T(8,128)(2,1)S(1)}, bf16[64,4096]{1,0:T(8,128)(2,1)S(1)}, u32[]{:S(2)}, u32[]{:S(2)}) %collective-permute-start.30) | collective-permute-done | bytes 524320 | tf_op jit(solution)/shard_map/ppermute | solution.py:25
  283.3 3.7 %last_sum.1 = bf16[32,8,2048]{2,1,0:T(8,128)(2,1)} custom-call(bf16[128,4096]{1,0:T(8,128)(2,1)} %add_convert_fusion.2.own_ref, bf16[64,4096]{1,0:T(8,128)(2,1)} %copy-done.6, bf16[64,4096]{1,0:T(8,128)(2,1)} %copy-done.8, bf16[64,4096]{1,0:T(8,128)(2,1)} %copy-done.9, bf16[64,4096]{1,0:T(8,128)(2,1)} %copy-done.7), custom_call_target="tpu_custom_call" | custom-call | flops 1048576 | bytes 4194304 | tf_op jit(solution)/shard_map/last_sum/pallas_call | solution.py:330
  287.0 8.9 %all-to-all-start.4 = ((bf16[32,8,2048]{2,1,0:T(8,128)(2,1)}), bf16[32,8,2048]{2,1,0:T(8,128)(2,1)S(1)}, u32[]{:S(2)}, u32[]{:S(2)}) async-start(bf16[32,8,2048]{2,1,0:T(8,128)(2,1)} %last_sum.1), calls=%async_computation.4 | async-start | bytes 2097152 | tf_op jit(solution)/shard_map/all_to_all | solution.py:416
  298.0 24.1 %all-to-all-done.4 = bf16[32,8,2048]{2,1,0:T(8,128)(2,1)S(1)} async-done(((bf16[32,8,2048]{2,1,0:T(8,128)(2,1)}), bf16[32,8,2048]{2,1,0:T(8,128)(2,1)S(1)}, u32[]{:S(2)}, u32[]{:S(2)}) %all-to-all-start.4) | async-done | bytes 1048608 | tf_op jit(solution)/shard_map/all_to_all | solution.py:416
  (144 shorter events, 45.5 us)
Async XLA Ops:
  4.5 65.4 %all-to-all-start = ((bf16[4,144,1152]{2,1,0:T(8,128)(2,1)}), bf16[4,144,1152]{2,1,0:T(8,128)(2,1)S(1)}, u32[]{:S(2)}, u32[]{:S(2)}) async-start(bf16[4,144,1152]{2,1,0:T(8,128)(2,1)} %pack.1), calls=%async_computation | async-start | bytes 2654208 | tf_op jit(solution)/shard_map/all_to_all | solution.py:378
  8.8 9.4 %collective-permute-start.8 = (bf16[1024,128]{1,0:T(8,128)(2,1)S(1)}, bf16[1024,128]{1,0:T(8,128)(2,1)S(1)}, u32[]{:S(2)}, u32[]{:S(2)}) collective-permute-start(bf16[1024,128]{1,0:T(8,128)(2,1)S(1)} %copy-done.17), channel_id=1, source_target_pairs={{0,32},{32,0},{1,33},{33,1},{2,34},{34,2},{3,35},{35,3},{4,36},{36... | collective-permute-start | bytes 786440 | tf_op jit(solution)/shard_map/ppermute | solution.py:25
  8.8 15.5 %collective-permute-start = (bf16[1024,128]{1,0:T(8,128)(2,1)S(1)}, bf16[1024,128]{1,0:T(8,128)(2,1)S(1)}, u32[]{:S(2)}, u32[]{:S(2)}) collective-permute-start(bf16[1024,128]{1,0:T(8,128)(2,1)S(1)} %copy-done.17), channel_id=1, source_target_pairs={{0,64},{64,128},{128,192},{192,0},{1,65},{65,129},{129,193},{193,1... | collective-permute-start | bytes 786440 | tf_op jit(solution)/shard_map/ppermute | solution.py:25
  12.2 22.9 %collective-permute-start.5 = (bf16[1024,128]{1,0:T(8,128)(2,1)S(1)}, bf16[1024,128]{1,0:T(8,128)(2,1)S(1)}, u32[]{:S(2)}, u32[]{:S(2)}) collective-permute-start(bf16[1024,128]{1,0:T(8,128)(2,1)S(1)} %copy-done.18), channel_id=1, source_target_pairs={{0,192},{64,0},{128,64},{192,128},{1,193},{65,1},{129,65},{193,129... | collective-permute-start | bytes 786440 | tf_op jit(solution)/shard_map/ppermute | solution.py:25
  15.3 24.8 %collective-permute-start.1 = (bf16[1024,128]{1,0:T(8,128)(2,1)S(1)}, bf16[1024,128]{1,0:T(8,128)(2,1)S(1)}, u32[]{:S(2)}, u32[]{:S(2)}) collective-permute-start(bf16[1024,128]{1,0:T(8,128)(2,1)S(1)} %copy-done.17), channel_id=1, source_target_pairs={{0,192},{64,0},{128,64},{192,128},{1,193},{65,1},{129,65},{193,129... | collective-permute-start | bytes 786440 | tf_op jit(solution)/shard_map/ppermute | solution.py:25
  18.1 22.0 %collective-permute-start.4 = (bf16[1024,128]{1,0:T(8,128)(2,1)S(1)}, bf16[1024,128]{1,0:T(8,128)(2,1)S(1)}, u32[]{:S(2)}, u32[]{:S(2)}) collective-permute-start(bf16[1024,128]{1,0:T(8,128)(2,1)S(1)} %copy-done.18), channel_id=1, source_target_pairs={{0,64},{64,128},{128,192},{192,0},{1,65},{65,129},{129,193},{193,1... | collective-permute-start | bytes 786440 | tf_op jit(solution)/shard_map/ppermute | solution.py:25
  18.2 22.4 %collective-permute-start.9 = (bf16[1024,128]{1,0:T(8,128)(2,1)S(1)}, bf16[1024,128]{1,0:T(8,128)(2,1)S(1)}, u32[]{:S(2)}, u32[]{:S(2)}) collective-permute-start(bf16[1024,128]{1,0:T(8,128)(2,1)S(1)} %copy-done.18), channel_id=1, source_target_pairs={{0,32},{32,0},{1,33},{33,1},{2,34},{34,2},{3,35},{35,3},{4,36},{36... | collective-permute-start | bytes 786440 | tf_op jit(solution)/shard_map/ppermute | solution.py:25
  24.4 20.0 %collective-permute-start.2 = (bf16[1024,128]{1,0:T(8,128)(2,1)S(1)}, bf16[1024,128]{1,0:T(8,128)(2,1)S(1)}, u32[]{:S(2)}, u32[]{:S(2)}) collective-permute-start(bf16[1024,128]{1,0:T(8,128)(2,1)S(1)} %collective-permute-done.refs_1_), channel_id=1, source_target_pairs={{0,32},{32,0},{1,33},{33,1},{2,34},{34,2},{3,35},{35,3},{4,36},{36... | collective-permute-start | bytes 786440 | tf_op jit(solution)/shard_map/ppermute | solution.py:25
  35.0 19.6 %collective-permute-start.7 = (bf16[1024,128]{1,0:T(8,128)(2,1)S(1)}, bf16[1024,128]{1,0:T(8,128)(2,1)}, u32[]{:S(2)}, u32[]{:S(2)}) collective-permute-start(bf16[1024,128]{1,0:T(8,128)(2,1)S(1)} %collective-permute-done.5.refs_6_), channel_id=1, source_target_pairs={{0,32},{32,0},{1,33},{33,1},{2,34},{34,2},{3,35},{35,3},{4,36},{36... | collective-permute-start | bytes 786440 | tf_op jit(solution)/shard_map/ppermute | solution.py:25
  40.1 14.6 %collective-permute-start.3 = (bf16[1024,128]{1,0:T(8,128)(2,1)S(1)}, bf16[1024,128]{1,0:T(8,128)(2,1)}, u32[]{:S(2)}, u32[]{:S(2)}) collective-permute-start(bf16[1024,128]{1,0:T(8,128)(2,1)S(1)} %collective-permute-done.1.refs_2_), channel_id=1, source_target_pairs={{0,32},{32,0},{1,33},{33,1},{2,34},{34,2},{3,35},{35,3},{4,36},{36... | collective-permute-start | bytes 786440 | tf_op jit(solution)/shard_map/ppermute | solution.py:25
  40.2 14.6 %collective-permute-start.6 = (bf16[1024,128]{1,0:T(8,128)(2,1)S(1)}, bf16[1024,128]{1,0:T(8,128)(2,1)}, u32[]{:S(2)}, u32[]{:S(2)}) collective-permute-start(bf16[1024,128]{1,0:T(8,128)(2,1)S(1)} %collective-permute-done.4.refs_5_), channel_id=1, source_target_pairs={{0,32},{32,0},{1,33},{33,1},{2,34},{34,2},{3,35},{35,3},{4,36},{36... | collective-permute-start | bytes 786440 | tf_op jit(solution)/shard_map/ppermute | solution.py:25
  40.7 31.9 %collective-permute-start.10 = (bf16[1024,128]{1,0:T(8,128)(2,1)S(1)}, bf16[1024,128]{1,0:T(8,128)(2,1)S(1)}, u32[]{:S(2)}, u32[]{:S(2)}) collective-permute-start(bf16[1024,128]{1,0:T(8,128)(2,1)S(1)} %collective-permute-done.refs_1_), channel_id=1, source_target_pairs={{0,64},{64,128},{128,192},{192,0},{1,65},{65,129},{129,193},{193,1... | collective-permute-start | bytes 786440 | tf_op jit(solution)/shard_map/ppermute | solution.py:25
  44.3 28.3 %collective-permute-start.11 = (bf16[1024,128]{1,0:T(8,128)(2,1)S(1)}, bf16[1024,128]{1,0:T(8,128)(2,1)S(1)}, u32[]{:S(2)}, u32[]{:S(2)}) collective-permute-start(bf16[1024,128]{1,0:T(8,128)(2,1)S(1)} %collective-permute-done.5.refs_6_), channel_id=1, source_target_pairs={{0,192},{64,0},{128,64},{192,128},{1,193},{65,1},{129,65},{193,129... | collective-permute-start | bytes 786440 | tf_op jit(solution)/shard_map/ppermute | solution.py:25
  88.1 7.9 %collective-permute-start.16 = (bf16[512,128]{1,0:T(8,128)(2,1)}, bf16[512,128]{1,0:T(8,128)(2,1)S(1)}, u32[]{:S(2)}, u32[]{:S(2)}) collective-permute-start(bf16[512,128]{1,0:T(8,128)(2,1)} %shard_map.109.refs_0_), channel_id=1, source_target_pairs={{0,16},{8,24},{16,0},{24,8},{1,17},{9,25},{17,1},{25,9},{2,18},{10... | collective-permute-start | bytes 393224 | tf_op jit(solution)/shard_map/ppermute | solution.py:25
  155.4 22.4 %collective-permute-start.19 = (bf16[128,4096]{1,0:T(8,128)(2,1)}, bf16[128,4096]{1,0:T(8,128)(2,1)}, u32[]{:S(2)}, u32[]{:S(2)}) collective-permute-start(bf16[128,4096]{1,0:T(8,128)(2,1)} %norm_rows.1.refs_0_), channel_id=1, source_target_pairs={{0,1},{1,2},{2,3},{3,0},{4,5},{5,6},{6,7},{7,4},{8,9},{9,10},{10,1... | collective-permute-start | bytes 3145736 | tf_op jit(solution)/shard_map/ppermute | solution.py:25
  155.6 23.5 %collective-permute-start.20 = (bf16[128,4096]{1,0:T(8,128)(2,1)}, bf16[128,4096]{1,0:T(8,128)(2,1)}, u32[]{:S(2)}, u32[]{:S(2)}) collective-permute-start(bf16[128,4096]{1,0:T(8,128)(2,1)} %norm_rows.1.refs_0_), channel_id=1, source_target_pairs={{0,3},{1,0},{2,1},{3,2},{4,7},{5,4},{6,5},{7,6},{8,11},{9,8},{10,9... | collective-permute-start | bytes 3145736 | tf_op jit(solution)/shard_map/ppermute | solution.py:25
  178.8 9.3 %collective-permute-start.24 = (bf16[64,4096]{1,0:T(8,128)(2,1)S(1)}, bf16[64,4096]{1,0:T(8,128)(2,1)S(1)}, u32[]{:S(2)}, u32[]{:S(2)}) collective-permute-start(bf16[64,4096]{1,0:T(8,128)(2,1)S(1)} %slice.33), channel_id=1, source_target_pairs={{0,1},{1,2},{2,3},{3,0},{4,5},{5,6},{6,7},{7,4},{8,9},{9,10},{10,1... | collective-permute-start | bytes 1572872 | tf_op jit(solution)/shard_map/ppermute | solution.py:25
  180.3 9.3 %collective-permute-start.25 = (bf16[64,4096]{1,0:T(8,128)(2,1)S(1)}, bf16[64,4096]{1,0:T(8,128)(2,1)S(1)}, u32[]{:S(2)}, u32[]{:S(2)}) collective-permute-start(bf16[64,4096]{1,0:T(8,128)(2,1)S(1)} %slice.34), channel_id=1, source_target_pairs={{0,3},{1,0},{2,1},{3,2},{4,7},{5,4},{6,5},{7,6},{8,11},{9,8},{10,9... | collective-permute-start | bytes 1572872 | tf_op jit(solution)/shard_map/ppermute | solution.py:25
  189.7 20.8 %collective-permute-start.21 = (bf16[128,4096]{1,0:T(8,128)(2,1)}, bf16[128,4096]{1,0:T(8,128)(2,1)}, u32[]{:S(2)}, u32[]{:S(2)}) collective-permute-start(bf16[128,4096]{1,0:T(8,128)(2,1)} %collective-permute-done.19.refs_0_), channel_id=1, source_target_pairs={{0,32},{32,0},{1,33},{33,1},{2,34},{34,2},{3,35},{35,3},{4,36},{36... | collective-permute-start | bytes 3145736 | tf_op jit(solution)/shard_map/ppermute | solution.py:25
  190.2 20.3 %collective-permute-start.22 = (bf16[128,4096]{1,0:T(8,128)(2,1)}, bf16[128,4096]{1,0:T(8,128)(2,1)}, u32[]{:S(2)}, u32[]{:S(2)}) collective-permute-start(bf16[128,4096]{1,0:T(8,128)(2,1)} %collective-permute-done.20.refs_1_), channel_id=1, source_target_pairs={{0,32},{32,0},{1,33},{33,1},{2,34},{34,2},{3,35},{35,3},{4,36},{36... | collective-permute-start | bytes 3145736 | tf_op jit(solution)/shard_map/ppermute | solution.py:25
  190.3 35.7 %collective-permute-start.17 = (bf16[128,4096]{1,0:T(8,128)(2,1)S(1)}, bf16[128,4096]{1,0:T(8,128)(2,1)}, u32[]{:S(2)}, u32[]{:S(2)}) collective-permute-start(bf16[128,4096]{1,0:T(8,128)(2,1)S(1)} %copy-done.1), channel_id=1, source_target_pairs={{0,32},{32,0},{1,33},{33,1},{2,34},{34,2},{3,35},{35,3},{4,36},{36... | collective-permute-start | bytes 3145736 | tf_op jit(solution)/shard_map/ppermute | solution.py:25
  205.2 32.9 %collective-permute-start.27 = (bf16[128,4096]{1,0:T(8,128)(2,1)}, bf16[128,4096]{1,0:T(8,128)(2,1)}, u32[]{:S(2)}, u32[]{:S(2)}) collective-permute-start(bf16[128,4096]{1,0:T(8,128)(2,1)} %get-tuple-element.45), channel_id=1, source_target_pairs={{0,32},{32,0},{1,33},{33,1},{2,34},{34,2},{3,35},{35,3},{4,36},{36... | collective-permute-start | bytes 3145736 | tf_op jit(solution)/shard_map/ppermute | solution.py:25
  205.3 81.7 %all-to-all-start.2 = ((bf16[4,16,1024]{2,1,0:T(8,128)(2,1)}), bf16[4,16,1024]{2,1,0:T(8,128)(2,1)S(1)}, u32[]{:S(2)}, u32[]{:S(2)}) async-start(bf16[4,16,1024]{2,1,0:T(8,128)(2,1)} %bitcast.6), calls=%async_computation.2 | async-start | bytes 262144 | tf_op jit(solution)/shard_map/all_to_all | solution.py:390
  225.8 16.4 %collective-permute-start.23 = (bf16[256,4096]{1,0:T(8,128)(2,1)}, bf16[256,4096]{1,0:T(8,128)(2,1)S(1)}, u32[]{:S(2)}, u32[]{:S(2)}) collective-permute-start(bf16[256,4096]{1,0:T(8,128)(2,1)} %get-tuple-element.43), channel_id=1, source_target_pairs={{0,32},{32,0},{1,33},{33,1},{2,34},{34,2},{3,35},{35,3},{4,36},{36... | collective-permute-start | bytes 6291464 | tf_op jit(solution)/shard_map/ppermute | solution.py:25
  237.7 22.9 %collective-permute-start.18 = (bf16[128,4096]{1,0:T(8,128)(2,1)}, bf16[128,4096]{1,0:T(8,128)(2,1)S(1)}, u32[]{:S(2)}, u32[]{:S(2)}) collective-permute-start(bf16[128,4096]{1,0:T(8,128)(2,1)} %get-tuple-element.41), channel_id=1, source_target_pairs={{0,32},{32,0},{1,33},{33,1},{2,34},{34,2},{3,35},{35,3},{4,36},{36... | collective-permute-start | bytes 3145736 | tf_op jit(solution)/shard_map/ppermute | solution.py:25
  240.1 14.0 %collective-permute-start.28 = (bf16[64,4096]{1,0:T(8,128)(2,1)S(1)}, bf16[64,4096]{1,0:T(8,128)(2,1)S(1)}, u32[]{:S(2)}, u32[]{:S(2)}) collective-permute-start(bf16[64,4096]{1,0:T(8,128)(2,1)S(1)} %get-tuple-element.51), channel_id=1, source_target_pairs={{0,1},{1,2},{2,3},{3,0},{4,5},{5,6},{6,7},{7,4},{8,9},{9,10},{10,1... | collective-permute-start | bytes 1572872 | tf_op jit(solution)/shard_map/ppermute | solution.py:25
  241.7 14.2 %collective-permute-start.32 = (bf16[64,4096]{1,0:T(8,128)(2,1)S(1)}, bf16[64,4096]{1,0:T(8,128)(2,1)S(1)}, u32[]{:S(2)}, u32[]{:S(2)}) collective-permute-start(bf16[64,4096]{1,0:T(8,128)(2,1)S(1)} %get-tuple-element.50), channel_id=1, source_target_pairs={{0,3},{1,0},{2,1},{3,2},{4,7},{5,4},{6,5},{7,6},{8,11},{9,8},{10,9... | collective-permute-start | bytes 1572872 | tf_op jit(solution)/shard_map/ppermute | solution.py:25
  256.2 14.9 %collective-permute-start.29 = (bf16[64,4096]{1,0:T(8,128)(2,1)S(1)}, bf16[64,4096]{1,0:T(8,128)(2,1)S(1)}, u32[]{:S(2)}, u32[]{:S(2)}) collective-permute-start(bf16[64,4096]{1,0:T(8,128)(2,1)S(1)} %get-tuple-element.47), channel_id=1, source_target_pairs={{0,1},{1,2},{2,3},{3,0},{4,5},{5,6},{6,7},{7,4},{8,9},{9,10},{10,1... | collective-permute-start | bytes 1572872 | tf_op jit(solution)/shard_map/ppermute | solution.py:25
  258.0 14.8 %collective-permute-start.33 = (bf16[64,4096]{1,0:T(8,128)(2,1)S(1)}, bf16[64,4096]{1,0:T(8,128)(2,1)S(1)}, u32[]{:S(2)}, u32[]{:S(2)}) collective-permute-start(bf16[64,4096]{1,0:T(8,128)(2,1)S(1)} %get-tuple-element.46), channel_id=1, source_target_pairs={{0,3},{1,0},{2,1},{3,2},{4,7},{5,4},{6,5},{7,6},{8,11},{9,8},{10,9... | collective-permute-start | bytes 1572872 | tf_op jit(solution)/shard_map/ppermute | solution.py:25
  258.4 23.4 %collective-permute-start.30 = (bf16[64,4096]{1,0:T(8,128)(2,1)S(1)}, bf16[64,4096]{1,0:T(8,128)(2,1)S(1)}, u32[]{:S(2)}, u32[]{:S(2)}) collective-permute-start(bf16[64,4096]{1,0:T(8,128)(2,1)S(1)} %get-tuple-element.49), channel_id=1, source_target_pairs={{0,3},{1,0},{2,1},{3,2},{4,7},{5,4},{6,5},{7,6},{8,11},{9,8},{10,9... | collective-permute-start | bytes 1572872 | tf_op jit(solution)/shard_map/ppermute | solution.py:25
  260.6 21.2 %collective-permute-start.31 = (bf16[64,4096]{1,0:T(8,128)(2,1)S(1)}, bf16[64,4096]{1,0:T(8,128)(2,1)S(1)}, u32[]{:S(2)}, u32[]{:S(2)}) collective-permute-start(bf16[64,4096]{1,0:T(8,128)(2,1)S(1)} %get-tuple-element.48), channel_id=1, source_target_pairs={{0,1},{1,2},{2,3},{3,0},{4,5},{5,6},{6,7},{7,4},{8,9},{9,10},{10,1... | collective-permute-start | bytes 1572872 | tf_op jit(solution)/shard_map/ppermute | solution.py:25
  287.0 35.0 %all-to-all-start.4 = ((bf16[32,8,2048]{2,1,0:T(8,128)(2,1)}), bf16[32,8,2048]{2,1,0:T(8,128)(2,1)S(1)}, u32[]{:S(2)}, u32[]{:S(2)}) async-start(bf16[32,8,2048]{2,1,0:T(8,128)(2,1)} %last_sum.1), calls=%async_computation.4 | async-start | bytes 2097152 | tf_op jit(solution)/shard_map/all_to_all | solution.py:416
  (35 other events, 342.6 us)
where the time goes:
time: 326 us; the launch traced here: 324 us
  waiting for transfers between devices  115 us (35%)
  Pallas kernels  87.2 us (27%)
  blocking collectives  51.2 us (16%)
  starting transfers between devices  51 us (16%)
  local copies, waits for them, and re-layouts  11.5 us (4%)
  other arithmetic  5.48 us (2%)
    ppermute x34, waiting for transfers between devices, shift(): lax.ppermute(value, axis, [(i, (i + step) % size) for i in range(size)])  91.2 us
    pallas_call x3, Pallas kernels, expert_block(): pl.pallas_call(functools.partial(expert_kernel, count), grid=(width // de...  38.9 us
    pallas_call x3, Pallas kernels, attend(): pl.pallas_call(functools.partial(attend_kernel, len(keys), not state, las...  33.4 us
    all_to_all x1, blocking collectives, on_device(): lax.all_to_all(outgoing, PLANE, split_axis=0, concat_axis=0, tiled=True)  32.9 us
    ppermute x34, starting transfers between devices, shift(): lax.ppermute(value, axis, [(i, (i + step) % size) for i in range(size)])  32.6 us
    all_to_all x1, waiting for transfers between devices, on_device(): lax.all_to_all(summed, PLANE, split_axis=0, concat_axis=0, tiled=True)  24.1 us
    all_to_all x1, blocking collectives, on_device(): lax.all_to_all(partial_rows.reshape(group, nx * rows, chunk), ('zlo', 'y'...  18.3 us
    all_to_all x1, starting transfers between devices, on_device(): lax.all_to_all(summed, PLANE, split_axis=0, concat_axis=0, tiled=True)  8.94 us
  transfers between devices with their start and end apart: 37, of which 18 were waited for; matrix products, arithmetic and copies ran while one was open for 3% of the time, Pallas kernels for 21%

commit v1 on v0

--- a/solution.py
+++ b/solution.py
@@ -16,7 +16,6 @@
 INTERPRET = False
 
 
-X_STEPS = (0, 1, -1, 2)
 DEEP = 512
 
 
@@ -81,7 +80,7 @@
 
 def attend(queries, keys, values, state, last):
     total_rows, width = queries.shape
-    rows = min(128, total_rows)
+    rows = min(256, total_rows)
     heads = width // DH
     whole = [pl.BlockSpec(k.shape, lambda i, h: (0, 0)) for k in keys + values]
     part = pl.BlockSpec((rows, width), lambda i, h: (i, 0))
@@ -109,6 +108,7 @@
     near_keys = [swap(keys), shift(keys, "zhi", 1), shift(keys, "zhi", -1)]
     near_values = [swap(values), shift(values, "zhi", 1), shift(values, "zhi", -1)]
     state = attend(queries, [keys, near_keys[0]], [values, near_values[0]], [], False)
+    state, early = lax.optimization_barrier((state, early))
     far_key = shift(near_keys[1], "zhi", 1)
     far_value = shift(near_values[2], "zhi", -1)
     state = attend(
@@ -118,7 +118,7 @@
         state,
         False,
     )
-    state, far_key, far_value, early = lax.optimization_barrier((state, far_key, far_value, early))
+    state, far_key, far_value = lax.optimization_barrier((state, far_key, far_value))
     (context,) = attend(queries, [far_key, swap(far_key)], [far_value, swap(far_value)], state, True)
     return context, early
 
@@ -191,24 +191,23 @@
     )(payload)
 
 
-def project_kernel(chunk, x_ref, payload_ref, *refs):
-    contexts, out_ref = refs[:-1], refs[-1]
-    nx, width = len(contexts), contexts[0].shape[1]
-    context = jnp.concatenate([r[...] for r in contexts], axis=1)
-    weights = [payload_ref[(x_ref[0] - step + nx) % nx, :width, :chunk] for step in X_STEPS]
-    weight = jnp.concatenate(weights, axis=0)
+def project_kernel(chunk, payload_ref, contexts_ref, out_ref):
+    nx, _, width = contexts_ref.shape
+    context = jnp.concatenate([contexts_ref[i] for i in range(nx)], axis=1)
+    weight = jnp.concatenate([payload_ref[i, :width, :chunk] for i in range(nx)], axis=0)
     out_ref[...] = jnp.dot(context, weight, preferred_element_type=jnp.float32).astype(jnp.bfloat16)
 
 
-def project(at_x, contexts, payload, chunk):
-    rows, width = contexts[0].shape
+def project(contexts, payload, chunk):
+    count, rows, width = contexts.shape
     part = min(256, rows)
-    count = len(contexts)
     return pl.pallas_call(
         functools.partial(project_kernel, chunk),
         grid=(rows // part,),
-        in_specs=[pl.BlockSpec(memory_space=pltpu.SMEM), pl.BlockSpec(payload.shape, lambda i: (0, 0, 0))]
-        + [pl.BlockSpec((part, width), lambda i: (i, 0))] * count,
+        in_specs=[
+            pl.BlockSpec(payload.shape, lambda i: (0, 0, 0)),
+            pl.BlockSpec((count, part, width), lambda i: (0, i, 0)),
+        ],
         out_specs=pl.BlockSpec((part, chunk), lambda i: (i, 0)),
         out_shape=jax.ShapeDtypeStruct((rows, chunk), jnp.bfloat16),
         cost_estimate=pl.CostEstimate(
@@ -218,7 +217,7 @@
         ),
         name="project",
         interpret=INTERPRET,
-    )(at_x, payload, *contexts)
+    )(payload, contexts)
 
 
 def norm_kernel(groups, chunks, in_ref, gain_ref, out_ref):
@@ -252,56 +251,50 @@
 def expert_kernel(count, *refs):
     own, other = refs[:count], refs[count : 2 * count]
     gate_up, down, own_out, other_out, acc = refs[2 * count :]
-    step = pl.program_id(0)
-    rows = jnp.concatenate([r[...] for r in own + other], axis=0)
-
-    @pl.when(step == 0)
-    def _():
-        acc[...] = jnp.zeros(acc.shape, jnp.float32)
-
-    acc[...] += jnp.dot(rows, gate_up[...], preferred_element_type=jnp.float32)
-
-    @pl.when(step == pl.num_programs(0) - 1)
-    def _():
-        width = down.shape[0]
-        half = own_out.shape[0]
-        gate = acc[:, :width]
-        hidden = (gate / (1.0 + jnp.exp(-gate)) * acc[:, width:]).astype(jnp.bfloat16)
-        part = min(512, down.shape[1])
-
-        def columns(i, carry):
-            at = pl.ds(pl.multiple_of(i * part, part), part)
-            out = jnp.dot(hidden, down[:, at], preferred_element_type=jnp.float32).astype(jnp.bfloat16)
-            own_out[:, at] = out[:half]
-            other_out[:, at] = out[half:]
-            return carry
-
-        lax.fori_loop(0, down.shape[1] // part, columns, 0)
+    width, whole = down.shape
+    deep, part = min(DEEP, whole), min(512, whole)
+    acc[...] = jnp.zeros(acc.shape, jnp.float32)
+
+    def accumulate(i, carry):
+        at = pl.ds(pl.multiple_of(i * deep, deep), deep)
+        rows = jnp.concatenate([r[:, at] for r in own + other], axis=0)
+        acc[...] += jnp.dot(rows, gate_up[at, :], preferred_element_type=jnp.float32)
+        return carry
+
+    lax.fori_loop(0, whole // deep, accumulate, 0)
+    half = own_out.shape[0]
+    gate = acc[:, :width]
+    hidden = (gate / (1.0 + jnp.exp(-gate)) * acc[:, width:]).astype(jnp.bfloat16)
+
+    def columns(i, carry):
+        at = pl.ds(pl.multiple_of(i * part, part), part)
+        out = jnp.dot(hidden, down[:, at], preferred_element_type=jnp.float32).astype(jnp.bfloat16)
+        own_out[:, at] = out[:half]
+        other_out[:, at] = out[half:]
+        return carry
+
+    lax.fori_loop(0, whole // part, columns, 0)
 
 
 def expert_block(own, other, gate_up, down_weight):
     count = len(own)
     rows, width = own[0].shape
-    deep = min(DEEP, width)
     total = 2 * count * rows
-    block = pl.BlockSpec((rows, deep), lambda i: (0, i))
     shape = (count * rows, width)
-    whole = pl.BlockSpec(shape, lambda i: (0, 0))
+    operands = [in_vmem(v) for v in (*own, *other, gate_up, down_weight)]
     out_own, out_other = pl.pallas_call(
         functools.partial(expert_kernel, count),
-        grid=(width // deep,),
-        in_specs=[block] * (2 * count)
-        + [pl.BlockSpec((deep, gate_up.shape[1]), lambda i: (i, 0)), pl.BlockSpec(down_weight.shape, lambda i: (0, 0))],
-        out_specs=[whole, whole],
+        in_specs=[pl.BlockSpec(memory_space=pltpu.VMEM)] * len(operands),
         out_shape=[jax.ShapeDtypeStruct(shape, jnp.bfloat16)] * 2,
         scratch_shapes=[pltpu.VMEM((total, gate_up.shape[1]), jnp.float32)],
+        compiler_params=pltpu.CompilerParams(vmem_limit_bytes=24 << 20),
         cost_estimate=pl.CostEstimate(
             flops=2 * total * (gate_up.size + down_weight.size),
             bytes_accessed=2 * (gate_up.size + down_weight.size + 2 * total * width),
             transcendentals=total * down_weight.shape[0],
         ),
         interpret=INTERPRET,
-    )(*own, *other, gate_up, down_weight)
+    )(*operands)
     return add_rounded(out_own, swap(out_other))
 
 
@@ -372,7 +365,6 @@
     group = nzlo * ny
     experts = nx * nzlo
 
-    at_x = lax.axis_index("x").astype(jnp.int32).reshape(1)
     ordered = queries.reshape(nx, group, rows, -1).transpose(1, 0, 2, 3).reshape(queries.shape)
     sent = pack(residual, expert_ids, out_weight)
     payload = lax.all_to_all(sent, "x", split_axis=0, concat_axis=0, tiled=True)
@@ -380,8 +372,8 @@
     context, (payload, residual_chunk, chosen) = attention(
         ordered, doc_keys, doc_values, (payload, residual_chunk, chosen)
     )
-    contexts = [context] + [shift(context, "x", step) for step in X_STEPS[1:]]
-    partial_rows = project(at_x, contexts, payload, chunk)
+    contexts = lax.all_gather(context, "x", axis=0, tiled=False)
+    partial_rows = project(contexts, payload, chunk)
     pieces = lax.all_to_all(
         partial_rows.reshape(group, nx * rows, chunk), ("zlo", "y"), split_axis=0, concat_axis=0, tiled=True
     )

time: 326 us -> 308 us (0.945)
  Pallas kernels: 87.2 us -> 63.4 us
  blocking collectives: 51.2 us -> 64.1 us
  starting transfers between devices: 51 us -> 42.6 us
  local copies, waits for them, and re-layouts: 11.5 us -> 18.3 us
  waiting for transfers between devices: 115 us -> 110 us
    all_gather x0 -> x1, blocking collectives: none -> 15.4 us  [on_device(): contexts = lax.all_gather(context, 'x', axis=0, tiled=False)]
    pallas_call x3, Pallas kernels: 38.9 us -> 24.4 us  [expert_block(): pl.pallas_call(functools.partial(expert_kernel, count), in_specs=[pl.Bloc...]
    pallas_call x3, Pallas kernels: 33.4 us -> 24.3 us  [attend(): pl.pallas_call(functools.partial(attend_kernel, len(keys), not state, las...]
    unnamed x62 -> x58, local copies, waits for them, and re-layouts: 6.8 us -> 13.6 us
    ppermute x34 -> x31, starting transfers between devices: 32.6 us -> 27.4 us  [shift(): lax.ppermute(value, axis, [(i, (i + step) % size) for i in range(size)])]
    ppermute x34 -> x31, waiting for transfers between devices: 91.2 us -> 86.1 us  [shift(): lax.ppermute(value, axis, [(i, (i + step) % size) for i in range(size)])]
  transfers between devices with their start and end apart: 37 -> 34, of which waited for: 18 -> 15; matrix products, arithmetic and copies ran while one was open for 3% -> 3% of each run, Pallas kernels for 21% -> 15%
where the time goes in v1:
time: 308 us; the launch traced here: 306 us
  waiting for transfers between devices  110 us (36%)
  blocking collectives  64.1 us (21%)
  Pallas kernels  63.4 us (21%)
  starting transfers between devices  42.6 us (14%)
  local copies, waits for them, and re-layouts  18.3 us (6%)
  other arithmetic  5.03 us (2%)
    ppermute x31, waiting for transfers between devices, shift(): lax.ppermute(value, axis, [(i, (i + step) % size) for i in range(size)])  86.1 us
    all_to_all x1, blocking collectives, on_device(): lax.all_to_all(outgoing, PLANE, split_axis=0, concat_axis=0, tiled=True)  31.8 us
    ppermute x31, starting transfers between devices, shift(): lax.ppermute(value, axis, [(i, (i + step) % size) for i in range(size)])  27.4 us
    pallas_call x3, Pallas kernels, expert_block(): pl.pallas_call(functools.partial(expert_kernel, count), in_specs=[pl.Bloc...  24.4 us
    pallas_call x3, Pallas kernels, attend(): pl.pallas_call(functools.partial(attend_kernel, len(keys), not state, las...  24.3 us
    all_to_all x1, waiting for transfers between devices, on_device(): lax.all_to_all(summed, PLANE, split_axis=0, concat_axis=0, tiled=True)  24.1 us
    all_to_all x1, blocking collectives, on_device(): lax.all_to_all(partial_rows.reshape(group, nx * rows, chunk), ('zlo', 'y'...  16.9 us
    all_gather x1, blocking collectives, on_device(): contexts = lax.all_gather(context, 'x', axis=0, tiled=False)  15.4 us
  transfers between devices with their start and end apart: 34, of which 15 were waited for; matrix products, arithmetic and copies ran while one was open for 3% of the time, Pallas kernels for 15%

profile of v1, /device:TPU:8, one launch (start us, length us, event | category | flops | bytes accessed | tf_op | source)
XLA Modules:
  0.0 305.7 jit_solution(7452804588268620126)
XLA Ops:
  2.0 2.5 pack.1
  4.5 4.3 %all-to-all-start = ((bf16[4,144,1152]{2,1,0:T(8,128)(2,1)}), bf16[4,144,1152]{2,1,0:T(8,128)(2,1)S(1)}, u32[]{:S(2)}, u32[]{:S(2)}) async-start(bf16[4,144,1152]{2,1,0:T(8,128)(2,1)} %pack.1), calls=%async_computation | async-start | bytes 2654208 | tf_op jit(solution)/shard_map/all_to_all | solution.py:370
  8.8 3.3 %collective-permute-start.2 = (bf16[1024,128]{1,0:T(8,128)(2,1)S(1)}, bf16[1024,128]{1,0:T(8,128)(2,1)S(1)}, u32[]{:S(2)}, u32[]{:S(2)}) collective-permute-start(bf16[1024,128]{1,0:T(8,128)(2,1)S(1)} %copy-done.15), channel_id=1, source_target_pairs={{0,64},{64,128},{128,192},{192,0},{1,65},{65,129},{129,193},{193,1... | collective-permute-start | bytes 786440 | tf_op jit(solution)/shard_map/ppermute | solution.py:24
  12.2 3.1 %collective-permute-start.7 = (bf16[1024,128]{1,0:T(8,128)(2,1)S(1)}, bf16[1024,128]{1,0:T(8,128)(2,1)S(1)}, u32[]{:S(2)}, u32[]{:S(2)}) collective-permute-start(bf16[1024,128]{1,0:T(8,128)(2,1)S(1)} %copy-done.16), channel_id=1, source_target_pairs={{0,192},{64,0},{128,64},{192,128},{1,193},{65,1},{129,65},{193,129... | collective-permute-start | bytes 786440 | tf_op jit(solution)/shard_map/ppermute | solution.py:24
  15.3 2.8 collective-permute-start.3
  18.2 6.1 %collective-permute-done.2.refs_1_ = bf16[1024,128]{1,0:T(8,128)(2,1)S(1)} collective-permute-done((bf16[1024,128]{1,0:T(8,128)(2,1)S(1)}, bf16[1024,128]{1,0:T(8,128)(2,1)S(1)}, u32[]{:S(2)}, u32[]{:S(2)}) %collective-permute-start.2) | collective-permute-done | bytes 262176 | tf_op jit(solution)/shard_map/ppermute | solution.py:24
  24.3 10.7 %collective-permute-done.7.refs_6_ = bf16[1024,128]{1,0:T(8,128)(2,1)S(1)} collective-permute-done((bf16[1024,128]{1,0:T(8,128)(2,1)S(1)}, bf16[1024,128]{1,0:T(8,128)(2,1)S(1)}, u32[]{:S(2)}, u32[]{:S(2)}) %collective-permute-start.7) | collective-permute-done | bytes 262176 | tf_op jit(solution)/shard_map/ppermute | solution.py:24
  35.0 5.1 %collective-permute-done.3.refs_2_ = bf16[1024,128]{1,0:T(8,128)(2,1)S(1)} collective-permute-done((bf16[1024,128]{1,0:T(8,128)(2,1)S(1)}, bf16[1024,128]{1,0:T(8,128)(2,1)S(1)}, u32[]{:S(2)}, u32[]{:S(2)}) %collective-permute-start.3) | collective-permute-done | bytes 262176 | tf_op jit(solution)/shard_map/ppermute | solution.py:24
  40.6 3.7 %collective-permute-start.10 = (bf16[1024,128]{1,0:T(8,128)(2,1)S(1)}, bf16[1024,128]{1,0:T(8,128)(2,1)S(1)}, u32[]{:S(2)}, u32[]{:S(2)}) collective-permute-start(bf16[1024,128]{1,0:T(8,128)(2,1)S(1)} %collective-permute-done.2.refs_1_), channel_id=1, source_target_pairs={{0,64},{64,128},{128,192},{192,0},{1,65},{65,129},{129,193},{193,1... | collective-permute-start | bytes 786440 | tf_op jit(solution)/shard_map/ppermute | solution.py:24
  45.5 6.6 %shard_map.107 = (f32[512,128]{1,0:T(8,128)}, f32[512,128]{1,0:T(8,128)}, f32[512,128]{1,0:T(8,128)}) custom-call(bf16[512,128]{1,0:T(8,128)(2,1)} %bitcast.34, bf16[1024,128]{1,0:T(8,128)(2,1)} %refs_1_.1, bf16[1024,128]{1,0:T(8,128)(2,1)} %copy-done.21, bf16[1024,128]{1,0:T(8,128)(2,1)} %refs_3_.1, bf16[1024,128]{1,0:T(8,128)(2,1)} %copy-done.25), custom_call_target="tpu_custom_call" | custom-call | flops 536870912 | bytes 1966080 | tf_op jit(solution)/shard_map/pallas_call | solution.py:92
  54.9 10.8 %shard_map.108 = (f32[512,128]{1,0:T(8,128)}, f32[512,128]{1,0:T(8,128)}, f32[512,128]{1,0:T(8,128)}) custom-call(bf16[512,128]{1,0:T(8,128)(2,1)} %bitcast.35, bf16[1024,128]{1,0:T(8,128)(2,1)} %copy-done.17, bf16[1024,128]{1,0:T(8,128)(2,1)} %copy-done.19, bf16[1024,128]{1,0:T(8,128)(2,1)} %copy-done.23, bf16[1024,128]{1,0:T(8,128)(2,1)} %collective-permute-done.5.refs_4_, ...), custom_call_target="tpu_custom_call" | custom-call | flops 1073741824 | bytes 3014656 | tf_op jit(solution)/shard_map/pallas_call | solution.py:92
  68.8 6.8 %shard_map.109 = bf16[512,128]{1,0:T(8,128)(2,1)} custom-call(bf16[512,128]{1,0:T(8,128)(2,1)} %bitcast.36, bf16[1024,128]{1,0:T(8,128)(2,1)} %copy-done.22, bf16[1024,128]{1,0:T(8,128)(2,1)} %copy-done.26, bf16[1024,128]{1,0:T(8,128)(2,1)} %copy-done.24, bf16[1024,128]{1,0:T(8,128)(2,1)} %copy-done.27, f32[512,128]{1,0:T(8,128)} %get-tuple-element.42.refs_5_, ...), custom_call_target="tpu_custom_call" | custom-call | flops 536870912 | bytes 1966080 | tf_op jit(solution)/shard_map/pallas_call | solution.py:92
  75.6 15.4 %all-gather = bf16[2048,128]{1,0:T(8,128)(2,1)} all-gather(bf16[512,128]{1,0:T(8,128)(2,1)} %shard_map.109), channel_id=2, replica_groups=mesh['zhi'=4,'core'=2,'x'=4,'zlo'=2,'y'=4] {'x'}, dimensions={0}, use_global_device_ids=true | all-gather | bytes 655360 | tf_op jit(solution)/shard_map/all_gather | solution.py:375
  91.0 3.1 %project.1 = bf16[512,1024]{1,0:T(8,128)(2,1)} custom-call(bf16[4,144,1152]{2,1,0:T(8,128)(2,1)} %copy-done.6, bf16[4,512,128]{2,1,0:T(8,128)(2,1)} %bitcast.30), custom_call_target="tpu_custom_call" | custom-call | flops 536870912 | bytes 2621440 | tf_op jit(solution)/shard_map/project/pallas_call | solution.py:204
  94.1 16.9 %all_to_all.39 = bf16[8,64,1024]{2,1,0:T(8,128)(2,1)S(1)} all-to-all(bf16[8,64,1024]{2,1,0:T(8,128)(2,1)} %bitcast.29), channel_id=1, replica_groups=mesh['zhi'=4,'core'=2,'x'=4,'zlo'=2,'y'=4] {'zlo','y'}, dimensions={0} | all-to-all | bytes 2097152 | tf_op jit(solution)/shard_map/all_to_all | solution.py:377
  113.1 31.8 %all_to_all.40.in_ref = bf16[32,16,1024]{2,1,0:T(8,128)(2,1)S(1)} all-to-all(bf16[32,16,1024]{2,1,0:T(8,128)(2,1)S(1)} %bitcast.28), channel_id=1, replica_groups=mesh['zhi'=4,'core'=2,'x'=4,'zlo'=2,'y'=4] {'zhi','zlo','x'}, dimensions={0} | all-to-all | bytes 2097152 | tf_op jit(solution)/shard_map/all_to_all | solution.py:389
  149.1 20.4 %collective-permute-done.16.refs_0_ = bf16[128,4096]{1,0:T(8,128)(2,1)} collective-permute-done((bf16[128,4096]{1,0:T(8,128)(2,1)}, bf16[128,4096]{1,0:T(8,128)(2,1)}, u32[]{:S(2)}, u32[]{:S(2)}) %collective-permute-start.16) | collective-permute-done | bytes 1048608 | tf_op jit(solution)/shard_map/ppermute | solution.py:24
  173.8 6.0 %collective-permute-done.21 = bf16[64,4096]{1,0:T(8,128)(2,1)S(1)} collective-permute-done((bf16[64,4096]{1,0:T(8,128)(2,1)S(1)}, bf16[64,4096]{1,0:T(8,128)(2,1)S(1)}, u32[]{:S(2)}, u32[]{:S(2)}) %collective-permute-start.21) | collective-permute-done | bytes 524320 | tf_op jit(solution)/shard_map/ppermute | solution.py:24
  183.9 2.5 copy-done
  186.4 6.6 %shard_map.112 = (bf16[128,4096]{1,0:T(8,128)(2,1)S(1)}, bf16[128,4096]{1,0:T(8,128)(2,1)}) custom-call(bf16[128,4096]{1,0:T(8,128)(2,1)S(1)} %constant_dynamic-update-slice_fusion.refs_0_, bf16[128,4096]{1,0:T(8,128)(2,1)S(1)} %collective-permute-done.23.refs_1_, bf16[4096,640]{1,0:T(8,128)(2,1)S(1)} %bitcast.21, bf16[320,4096]{1,0:T(8,128)(2,1)S(1)} %bitcast.24), custom_call_target="tpu_custom_call" | custom-call | flops 2013265920 | bytes 12058624 | tf_op jit(solution)/shard_map/pallas_call | solution.py:285
  194.2 4.4 %all-to-all-start.2 = ((bf16[4,16,1024]{2,1,0:T(8,128)(2,1)}), bf16[4,16,1024]{2,1,0:T(8,128)(2,1)S(1)}, u32[]{:S(2)}, u32[]{:S(2)}) async-start(bf16[4,16,1024]{2,1,0:T(8,128)(2,1)} %bitcast.6), calls=%async_computation.2 | async-start | bytes 262144 | tf_op jit(solution)/shard_map/all_to_all | solution.py:382
  198.6 2.5 copy-done.1
  201.1 10.6 %shard_map.111 = (bf16[256,4096]{1,0:T(8,128)(2,1)S(1)}, bf16[256,4096]{1,0:T(8,128)(2,1)S(1)}) custom-call(bf16[128,4096]{1,0:T(8,128)(2,1)} %collective-permute-done.16.refs_0_, bf16[128,4096]{1,0:T(8,128)(2,1)} %collective-permute-done.17.refs_1_, bf16[128,4096]{1,0:T(8,128)(2,1)} %collective-permute-done.18.refs_2_, ...), custom_call_target="tpu_custom_call" | custom-call | flops 4026531840 | bytes 16252928 | tf_op jit(solution)/shard_map/pallas_call | solution.py:285
  212.1 2.5 copy-done.2
  214.6 7.2 %shard_map.110 = (bf16[128,4096]{1,0:T(8,128)(2,1)S(1)}, bf16[128,4096]{1,0:T(8,128)(2,1)S(1)}) custom-call(bf16[128,4096]{1,0:T(8,128)(2,1)} %norm_rows.1.refs_0_, bf16[128,4096]{1,0:T(8,128)(2,1)} %collective-permute-done.14.refs_1_, bf16[4096,640]{1,0:T(8,128)(2,1)S(1)} %bitcast.23, bf16[320,4096]{1,0:T(8,128)(2,1)S(1)} %bitcast.26), custom_call_target="tpu_custom_call" | custom-call | flops 2013265920 | bytes 12058624 | tf_op jit(solution)/shard_map/pallas_call | solution.py:285
  226.8 11.1 %collective-permute-done.25 = bf16[64,4096]{1,0:T(8,128)(2,1)S(1)} collective-permute-done((bf16[64,4096]{1,0:T(8,128)(2,1)S(1)}, bf16[64,4096]{1,0:T(8,128)(2,1)S(1)}, u32[]{:S(2)}, u32[]{:S(2)}) %collective-permute-start.25) | collective-permute-done | bytes 524320 | tf_op jit(solution)/shard_map/ppermute | solution.py:24
  237.9 2.3 collective-permute-done.29
  246.1 9.3 %collective-permute-done.26.low_a = bf16[64,4096]{1,0:T(8,128)(2,1)S(1)} collective-permute-done((bf16[64,4096]{1,0:T(8,128)(2,1)S(1)}, bf16[64,4096]{1,0:T(8,128)(2,1)S(1)}, u32[]{:S(2)}, u32[]{:S(2)}) %collective-permute-start.26) | collective-permute-done | bytes 524320 | tf_op jit(solution)/shard_map/ppermute | solution.py:24
  257.1 9.1 %collective-permute-done.27.low_b = bf16[64,4096]{1,0:T(8,128)(2,1)S(1)} collective-permute-done((bf16[64,4096]{1,0:T(8,128)(2,1)S(1)}, bf16[64,4096]{1,0:T(8,128)(2,1)S(1)}, u32[]{:S(2)}, u32[]{:S(2)}) %collective-permute-start.27) | collective-permute-done | bytes 524320 | tf_op jit(solution)/shard_map/ppermute | solution.py:24
  267.7 3.7 %last_sum.1 = bf16[32,8,2048]{2,1,0:T(8,128)(2,1)} custom-call(bf16[128,4096]{1,0:T(8,128)(2,1)} %add_convert_fusion.2.own_ref, bf16[64,4096]{1,0:T(8,128)(2,1)} %copy-done.7, bf16[64,4096]{1,0:T(8,128)(2,1)} %copy-done.9, bf16[64,4096]{1,0:T(8,128)(2,1)} %copy-done.10, bf16[64,4096]{1,0:T(8,128)(2,1)} %copy-done.8), custom_call_target="tpu_custom_call" | custom-call | flops 1048576 | bytes 4194304 | tf_op jit(solution)/shard_map/last_sum/pallas_call | solution.py:323
  271.4 6.5 %all-to-all-start.4 = ((bf16[32,8,2048]{2,1,0:T(8,128)(2,1)}), bf16[32,8,2048]{2,1,0:T(8,128)(2,1)S(1)}, u32[]{:S(2)}, u32[]{:S(2)}) async-start(bf16[32,8,2048]{2,1,0:T(8,128)(2,1)} %last_sum.1), calls=%async_computation.4 | async-start | bytes 2097152 | tf_op jit(solution)/shard_map/all_to_all | solution.py:408
  279.9 24.1 %all-to-all-done.4 = bf16[32,8,2048]{2,1,0:T(8,128)(2,1)S(1)} async-done(((bf16[32,8,2048]{2,1,0:T(8,128)(2,1)}), bf16[32,8,2048]{2,1,0:T(8,128)(2,1)S(1)}, u32[]{:S(2)}, u32[]{:S(2)}) %all-to-all-start.4) | async-done | bytes 1048608 | tf_op jit(solution)/shard_map/all_to_all | solution.py:408
  (135 shorter events, 43.0 us)
Async XLA Ops:
  4.5 47.7 %all-to-all-start = ((bf16[4,144,1152]{2,1,0:T(8,128)(2,1)}), bf16[4,144,1152]{2,1,0:T(8,128)(2,1)S(1)}, u32[]{:S(2)}, u32[]{:S(2)}) async-start(bf16[4,144,1152]{2,1,0:T(8,128)(2,1)} %pack.1), calls=%async_computation | async-start | bytes 2654208 | tf_op jit(solution)/shard_map/all_to_all | solution.py:370
  8.8 9.4 %collective-permute-start = (bf16[1024,128]{1,0:T(8,128)(2,1)S(1)}, bf16[1024,128]{1,0:T(8,128)(2,1)S(1)}, u32[]{:S(2)}, u32[]{:S(2)}) collective-permute-start(bf16[1024,128]{1,0:T(8,128)(2,1)S(1)} %copy-done.15), channel_id=1, source_target_pairs={{0,32},{32,0},{1,33},{33,1},{2,34},{34,2},{3,35},{35,3},{4,36},{36... | collective-permute-start | bytes 786440 | tf_op jit(solution)/shard_map/ppermute | solution.py:24
  8.8 15.5 %collective-permute-start.2 = (bf16[1024,128]{1,0:T(8,128)(2,1)S(1)}, bf16[1024,128]{1,0:T(8,128)(2,1)S(1)}, u32[]{:S(2)}, u32[]{:S(2)}) collective-permute-start(bf16[1024,128]{1,0:T(8,128)(2,1)S(1)} %copy-done.15), channel_id=1, source_target_pairs={{0,64},{64,128},{128,192},{192,0},{1,65},{65,129},{129,193},{193,1... | collective-permute-start | bytes 786440 | tf_op jit(solution)/shard_map/ppermute | solution.py:24
  12.2 22.9 %collective-permute-start.7 = (bf16[1024,128]{1,0:T(8,128)(2,1)S(1)}, bf16[1024,128]{1,0:T(8,128)(2,1)S(1)}, u32[]{:S(2)}, u32[]{:S(2)}) collective-permute-start(bf16[1024,128]{1,0:T(8,128)(2,1)S(1)} %copy-done.16), channel_id=1, source_target_pairs={{0,192},{64,0},{128,64},{192,128},{1,193},{65,1},{129,65},{193,129... | collective-permute-start | bytes 786440 | tf_op jit(solution)/shard_map/ppermute | solution.py:24
  15.3 24.8 %collective-permute-start.3 = (bf16[1024,128]{1,0:T(8,128)(2,1)S(1)}, bf16[1024,128]{1,0:T(8,128)(2,1)S(1)}, u32[]{:S(2)}, u32[]{:S(2)}) collective-permute-start(bf16[1024,128]{1,0:T(8,128)(2,1)S(1)} %copy-done.15), channel_id=1, source_target_pairs={{0,192},{64,0},{128,64},{192,128},{1,193},{65,1},{129,65},{193,129... | collective-permute-start | bytes 786440 | tf_op jit(solution)/shard_map/ppermute | solution.py:24
  18.1 22.0 %collective-permute-start.6 = (bf16[1024,128]{1,0:T(8,128)(2,1)S(1)}, bf16[1024,128]{1,0:T(8,128)(2,1)S(1)}, u32[]{:S(2)}, u32[]{:S(2)}) collective-permute-start(bf16[1024,128]{1,0:T(8,128)(2,1)S(1)} %copy-done.16), channel_id=1, source_target_pairs={{0,64},{64,128},{128,192},{192,0},{1,65},{65,129},{129,193},{193,1... | collective-permute-start | bytes 786440 | tf_op jit(solution)/shard_map/ppermute | solution.py:24
  18.2 22.4 %collective-permute-start.1 = (bf16[1024,128]{1,0:T(8,128)(2,1)S(1)}, bf16[1024,128]{1,0:T(8,128)(2,1)S(1)}, u32[]{:S(2)}, u32[]{:S(2)}) collective-permute-start(bf16[1024,128]{1,0:T(8,128)(2,1)S(1)} %copy-done.16), channel_id=1, source_target_pairs={{0,32},{32,0},{1,33},{33,1},{2,34},{34,2},{3,35},{35,3},{4,36},{36... | collective-permute-start | bytes 786440 | tf_op jit(solution)/shard_map/ppermute | solution.py:24
  24.3 20.0 %collective-permute-start.4 = (bf16[1024,128]{1,0:T(8,128)(2,1)S(1)}, bf16[1024,128]{1,0:T(8,128)(2,1)S(1)}, u32[]{:S(2)}, u32[]{:S(2)}) collective-permute-start(bf16[1024,128]{1,0:T(8,128)(2,1)S(1)} %collective-permute-done.2.refs_1_), channel_id=1, source_target_pairs={{0,32},{32,0},{1,33},{33,1},{2,34},{34,2},{3,35},{35,3},{4,36},{36... | collective-permute-start | bytes 786440 | tf_op jit(solution)/shard_map/ppermute | solution.py:24
  35.0 19.9 %collective-permute-start.9 = (bf16[1024,128]{1,0:T(8,128)(2,1)S(1)}, bf16[1024,128]{1,0:T(8,128)(2,1)}, u32[]{:S(2)}, u32[]{:S(2)}) collective-permute-start(bf16[1024,128]{1,0:T(8,128)(2,1)S(1)} %collective-permute-done.7.refs_6_), channel_id=1, source_target_pairs={{0,32},{32,0},{1,33},{33,1},{2,34},{34,2},{3,35},{35,3},{4,36},{36... | collective-permute-start | bytes 786440 | tf_op jit(solution)/shard_map/ppermute | solution.py:24
  40.1 14.8 %collective-permute-start.5 = (bf16[1024,128]{1,0:T(8,128)(2,1)S(1)}, bf16[1024,128]{1,0:T(8,128)(2,1)}, u32[]{:S(2)}, u32[]{:S(2)}) collective-permute-start(bf16[1024,128]{1,0:T(8,128)(2,1)S(1)} %collective-permute-done.3.refs_2_), channel_id=1, source_target_pairs={{0,32},{32,0},{1,33},{33,1},{2,34},{34,2},{3,35},{35,3},{4,36},{36... | collective-permute-start | bytes 786440 | tf_op jit(solution)/shard_map/ppermute | solution.py:24
  40.1 14.8 %collective-permute-start.8 = (bf16[1024,128]{1,0:T(8,128)(2,1)S(1)}, bf16[1024,128]{1,0:T(8,128)(2,1)}, u32[]{:S(2)}, u32[]{:S(2)}) collective-permute-start(bf16[1024,128]{1,0:T(8,128)(2,1)S(1)} %collective-permute-done.6.refs_5_), channel_id=1, source_target_pairs={{0,32},{32,0},{1,33},{33,1},{2,34},{34,2},{3,35},{35,3},{4,36},{36... | collective-permute-start | bytes 786440 | tf_op jit(solution)/shard_map/ppermute | solution.py:24
  40.6 25.1 %collective-permute-start.10 = (bf16[1024,128]{1,0:T(8,128)(2,1)S(1)}, bf16[1024,128]{1,0:T(8,128)(2,1)S(1)}, u32[]{:S(2)}, u32[]{:S(2)}) collective-permute-start(bf16[1024,128]{1,0:T(8,128)(2,1)S(1)} %collective-permute-done.2.refs_1_), channel_id=1, source_target_pairs={{0,64},{64,128},{128,192},{192,0},{1,65},{65,129},{129,193},{193,1... | collective-permute-start | bytes 786440 | tf_op jit(solution)/shard_map/ppermute | solution.py:24
  44.3 21.4 %collective-permute-start.11 = (bf16[1024,128]{1,0:T(8,128)(2,1)S(1)}, bf16[1024,128]{1,0:T(8,128)(2,1)S(1)}, u32[]{:S(2)}, u32[]{:S(2)}) collective-permute-start(bf16[1024,128]{1,0:T(8,128)(2,1)S(1)} %collective-permute-done.7.refs_6_), channel_id=1, source_target_pairs={{0,192},{64,0},{128,64},{192,128},{1,193},{65,1},{129,65},{193,129... | collective-permute-start | bytes 786440 | tf_op jit(solution)/shard_map/ppermute | solution.py:24
  147.1 22.4 %collective-permute-start.16 = (bf16[128,4096]{1,0:T(8,128)(2,1)}, bf16[128,4096]{1,0:T(8,128)(2,1)}, u32[]{:S(2)}, u32[]{:S(2)}) collective-permute-start(bf16[128,4096]{1,0:T(8,128)(2,1)} %norm_rows.1.refs_0_), channel_id=1, source_target_pairs={{0,1},{1,2},{2,3},{3,0},{4,5},{5,6},{6,7},{7,4},{8,9},{9,10},{10,1... | collective-permute-start | bytes 3145736 | tf_op jit(solution)/shard_map/ppermute | solution.py:24
  147.3 23.5 %collective-permute-start.17 = (bf16[128,4096]{1,0:T(8,128)(2,1)}, bf16[128,4096]{1,0:T(8,128)(2,1)}, u32[]{:S(2)}, u32[]{:S(2)}) collective-permute-start(bf16[128,4096]{1,0:T(8,128)(2,1)} %norm_rows.1.refs_0_), channel_id=1, source_target_pairs={{0,3},{1,0},{2,1},{3,2},{4,7},{5,4},{6,5},{7,6},{8,11},{9,8},{10,9... | collective-permute-start | bytes 3145736 | tf_op jit(solution)/shard_map/ppermute | solution.py:24
  170.5 9.3 %collective-permute-start.21 = (bf16[64,4096]{1,0:T(8,128)(2,1)S(1)}, bf16[64,4096]{1,0:T(8,128)(2,1)S(1)}, u32[]{:S(2)}, u32[]{:S(2)}) collective-permute-start(bf16[64,4096]{1,0:T(8,128)(2,1)S(1)} %slice.33), channel_id=1, source_target_pairs={{0,1},{1,2},{2,3},{3,0},{4,5},{5,6},{6,7},{7,4},{8,9},{9,10},{10,1... | collective-permute-start | bytes 1572872 | tf_op jit(solution)/shard_map/ppermute | solution.py:24
  171.9 9.3 %collective-permute-start.22 = (bf16[64,4096]{1,0:T(8,128)(2,1)S(1)}, bf16[64,4096]{1,0:T(8,128)(2,1)S(1)}, u32[]{:S(2)}, u32[]{:S(2)}) collective-permute-start(bf16[64,4096]{1,0:T(8,128)(2,1)S(1)} %slice.34), channel_id=1, source_target_pairs={{0,3},{1,0},{2,1},{3,2},{4,7},{5,4},{6,5},{7,6},{8,11},{9,8},{10,9... | collective-permute-start | bytes 1572872 | tf_op jit(solution)/shard_map/ppermute | solution.py:24
  181.2 2.7 collective-permute-start.23
  181.3 17.3 %collective-permute-start.18 = (bf16[128,4096]{1,0:T(8,128)(2,1)}, bf16[128,4096]{1,0:T(8,128)(2,1)}, u32[]{:S(2)}, u32[]{:S(2)}) collective-permute-start(bf16[128,4096]{1,0:T(8,128)(2,1)} %collective-permute-done.16.refs_0_), channel_id=1, source_target_pairs={{0,32},{32,0},{1,33},{33,1},{2,34},{34,2},{3,35},{35,3},{4,36},{36... | collective-permute-start | bytes 3145736 | tf_op jit(solution)/shard_map/ppermute | solution.py:24
  181.8 16.8 %collective-permute-start.19 = (bf16[128,4096]{1,0:T(8,128)(2,1)}, bf16[128,4096]{1,0:T(8,128)(2,1)}, u32[]{:S(2)}, u32[]{:S(2)}) collective-permute-start(bf16[128,4096]{1,0:T(8,128)(2,1)} %collective-permute-done.17.refs_1_), channel_id=1, source_target_pairs={{0,32},{32,0},{1,33},{33,1},{2,34},{34,2},{3,35},{35,3},{4,36},{36... | collective-permute-start | bytes 3145736 | tf_op jit(solution)/shard_map/ppermute | solution.py:24
  181.9 30.2 %collective-permute-start.14 = (bf16[128,4096]{1,0:T(8,128)(2,1)}, bf16[128,4096]{1,0:T(8,128)(2,1)}, u32[]{:S(2)}, u32[]{:S(2)}) collective-permute-start(bf16[128,4096]{1,0:T(8,128)(2,1)} %norm_rows.1.refs_0_), channel_id=1, source_target_pairs={{0,32},{32,0},{1,33},{33,1},{2,34},{34,2},{3,35},{35,3},{4,36},{36... | collective-permute-start | bytes 3145736 | tf_op jit(solution)/shard_map/ppermute | solution.py:24
  194.0 28.3 %collective-permute-start.24 = (bf16[128,4096]{1,0:T(8,128)(2,1)}, bf16[128,4096]{1,0:T(8,128)(2,1)}, u32[]{:S(2)}, u32[]{:S(2)}) collective-permute-start(bf16[128,4096]{1,0:T(8,128)(2,1)} %get-tuple-element.51), channel_id=1, source_target_pairs={{0,32},{32,0},{1,33},{33,1},{2,34},{34,2},{3,35},{35,3},{4,36},{36... | collective-permute-start | bytes 3145736 | tf_op jit(solution)/shard_map/ppermute | solution.py:24
  194.2 77.3 %all-to-all-start.2 = ((bf16[4,16,1024]{2,1,0:T(8,128)(2,1)}), bf16[4,16,1024]{2,1,0:T(8,128)(2,1)S(1)}, u32[]{:S(2)}, u32[]{:S(2)}) async-start(bf16[4,16,1024]{2,1,0:T(8,128)(2,1)} %bitcast.6), calls=%async_computation.2 | async-start | bytes 262144 | tf_op jit(solution)/shard_map/all_to_all | solution.py:382
  211.7 14.3 %collective-permute-start.20 = (bf16[256,4096]{1,0:T(8,128)(2,1)S(1)}, bf16[256,4096]{1,0:T(8,128)(2,1)S(1)}, u32[]{:S(2)}, u32[]{:S(2)}) collective-permute-start(bf16[256,4096]{1,0:T(8,128)(2,1)S(1)} %get-tuple-element.49), channel_id=1, source_target_pairs={{0,32},{32,0},{1,33},{33,1},{2,34},{34,2},{3,35},{35,3},{4,36},{36... | collective-permute-start | bytes 6291464 | tf_op jit(solution)/shard_map/ppermute | solution.py:24
  221.8 23.0 %collective-permute-start.15 = (bf16[128,4096]{1,0:T(8,128)(2,1)S(1)}, bf16[128,4096]{1,0:T(8,128)(2,1)S(1)}, u32[]{:S(2)}, u32[]{:S(2)}) collective-permute-start(bf16[128,4096]{1,0:T(8,128)(2,1)S(1)} %get-tuple-element.47), channel_id=1, source_target_pairs={{0,32},{32,0},{1,33},{33,1},{2,34},{34,2},{3,35},{35,3},{4,36},{36... | collective-permute-start | bytes 3145736 | tf_op jit(solution)/shard_map/ppermute | solution.py:24
  223.9 14.0 %collective-permute-start.25 = (bf16[64,4096]{1,0:T(8,128)(2,1)S(1)}, bf16[64,4096]{1,0:T(8,128)(2,1)S(1)}, u32[]{:S(2)}, u32[]{:S(2)}) collective-permute-start(bf16[64,4096]{1,0:T(8,128)(2,1)S(1)} %get-tuple-element.57), channel_id=1, source_target_pairs={{0,1},{1,2},{2,3},{3,0},{4,5},{5,6},{6,7},{7,4},{8,9},{9,10},{10,1... | collective-permute-start | bytes 1572872 | tf_op jit(solution)/shard_map/ppermute | solution.py:24
  225.7 14.5 %collective-permute-start.29 = (bf16[64,4096]{1,0:T(8,128)(2,1)S(1)}, bf16[64,4096]{1,0:T(8,128)(2,1)S(1)}, u32[]{:S(2)}, u32[]{:S(2)}) collective-permute-start(bf16[64,4096]{1,0:T(8,128)(2,1)S(1)} %get-tuple-element.56), channel_id=1, source_target_pairs={{0,3},{1,0},{2,1},{3,2},{4,7},{5,4},{6,5},{7,6},{8,11},{9,8},{10,9... | collective-permute-start | bytes 1572872 | tf_op jit(solution)/shard_map/ppermute | solution.py:24
  240.5 14.9 %collective-permute-start.26 = (bf16[64,4096]{1,0:T(8,128)(2,1)S(1)}, bf16[64,4096]{1,0:T(8,128)(2,1)S(1)}, u32[]{:S(2)}, u32[]{:S(2)}) collective-permute-start(bf16[64,4096]{1,0:T(8,128)(2,1)S(1)} %get-tuple-element.53), channel_id=1, source_target_pairs={{0,1},{1,2},{2,3},{3,0},{4,5},{5,6},{6,7},{7,4},{8,9},{9,10},{10,1... | collective-permute-start | bytes 1572872 | tf_op jit(solution)/shard_map/ppermute | solution.py:24
  242.3 14.8 %collective-permute-start.30 = (bf16[64,4096]{1,0:T(8,128)(2,1)S(1)}, bf16[64,4096]{1,0:T(8,128)(2,1)S(1)}, u32[]{:S(2)}, u32[]{:S(2)}) collective-permute-start(bf16[64,4096]{1,0:T(8,128)(2,1)S(1)} %get-tuple-element.52), channel_id=1, source_target_pairs={{0,3},{1,0},{2,1},{3,2},{4,7},{5,4},{6,5},{7,6},{8,11},{9,8},{10,9... | collective-permute-start | bytes 1572872 | tf_op jit(solution)/shard_map/ppermute | solution.py:24
  242.6 23.5 %collective-permute-start.27 = (bf16[64,4096]{1,0:T(8,128)(2,1)S(1)}, bf16[64,4096]{1,0:T(8,128)(2,1)S(1)}, u32[]{:S(2)}, u32[]{:S(2)}) collective-permute-start(bf16[64,4096]{1,0:T(8,128)(2,1)S(1)} %get-tuple-element.55), channel_id=1, source_target_pairs={{0,3},{1,0},{2,1},{3,2},{4,7},{5,4},{6,5},{7,6},{8,11},{9,8},{10,9... | collective-permute-start | bytes 1572872 | tf_op jit(solution)/shard_map/ppermute | solution.py:24
  244.8 21.3 %collective-permute-start.28 = (bf16[64,4096]{1,0:T(8,128)(2,1)S(1)}, bf16[64,4096]{1,0:T(8,128)(2,1)S(1)}, u32[]{:S(2)}, u32[]{:S(2)}) collective-permute-start(bf16[64,4096]{1,0:T(8,128)(2,1)S(1)} %get-tuple-element.54), channel_id=1, source_target_pairs={{0,1},{1,2},{2,3},{3,0},{4,5},{5,6},{6,7},{7,4},{8,9},{9,10},{10,1... | collective-permute-start | bytes 1572872 | tf_op jit(solution)/shard_map/ppermute | solution.py:24
  271.4 32.6 %all-to-all-start.4 = ((bf16[32,8,2048]{2,1,0:T(8,128)(2,1)}), bf16[32,8,2048]{2,1,0:T(8,128)(2,1)S(1)}, u32[]{:S(2)}, u32[]{:S(2)}) async-start(bf16[32,8,2048]{2,1,0:T(8,128)(2,1)} %last_sum.1), calls=%async_computation.4 | async-start | bytes 2097152 | tf_op jit(solution)/shard_map/all_to_all | solution.py:408
  (30 other events, 293.9 us)
